TPU v7x, 32 devices: a whole 2x2x4 slice. The times are simulated.
32 devices in a mesh: member: 8 (over y, x, core), band: 4 (over z).
Axes of the slice: x: 2, y: 2, z: 4, core: 2. Of those that a mesh axis runs over, the one named last changes fastest.
Arguments:
- controls: float32 [16, 16, 256, 512], P('member', None, 'band'), may hold values from -6 to 6
- members: float32 [16, 16, 256, 512], P('member', None, 'band'), may hold values from -6 to 6
- loc_lon: float32 [512, 512], replicated, may hold values from -0.25 to 0.25
- loc_lat: float32 [256, 256], replicated, may hold values from -0.375 to 0.375
- balance: float32 [5, 1024, 2048], P(None, 'band', 'member'), may hold values from -1 to 1
- innovation: float32 [16, 1024, 2048], P(None, 'band', 'member'), may hold values from -6 to 6
- obs_weight: float32 [16, 1024, 2048], P(None, 'band', 'member'), may hold values from 0.2 to 5
Outputs:
- gradient: float32 [16, 16, 256, 512], P('member', None, 'band')
All inputs are finite; a program needn't handle non-finite values.
Results may differ from a plain program's by a relative error of at most 0.00012.
Values sent between devices are 32-bit elements; how exact they have to be, the bound alone decides.
No kernel may reach another device: no remote copies, remote signals or barrier semaphores. Data moves between devices by JAX's collectives and lax.ppermute only.
A program may use at most 128 MiB of HBM per device.

v0:
```python
import functools
import math

import jax
import jax.numpy as jnp
import numpy as np
from jax import lax
from jax.experimental import pallas as pl
from jax.experimental.pallas import tpu as pltpu
from jax.sharding import PartitionSpec as P


F32, BF16 = jnp.float32, jnp.bfloat16
phase_fraction = (0.625, 0.875, 0.125, 0.375)
phase_start = (0, 0, 1, 1)
NN = (((1,), (0,)), ((), ()))
NT = (((1,), (1,)), ((), ()))


def cubic_weights(fraction):
    return (
        (-(fraction**3) + 2 * fraction**2 - fraction) / 2,
        (3 * fraction**3 - 5 * fraction**2 + 2) / 2,
        (-3 * fraction**3 + 4 * fraction**2 + fraction) / 2,
        (fraction**3 - fraction**2) / 2,
    )


def round_up(value, step):
    return -(-value // step) * step


def edged_matrix(coarse, rows_out, cols_out):
    matrix = np.zeros((rows_out, cols_out), np.float32)
    fine = 4 * coarse
    for row, at in [(i, i) for i in range(fine + 1)] + [(-1, rows_out - 1)]:
        cell, phase = divmod(row, 4)
        for tap, weight in enumerate(cubic_weights(phase_fraction[phase])):
            matrix[at, cell + phase_start[phase] + tap] += weight
    return matrix


def split(value):
    high = value.astype(BF16)
    return high, (value - high.astype(F32)).astype(BF16)


def outer_split(value):
    high = lax.reduce_precision(value, 8, 7)
    return high.astype(BF16), lax.reduce_precision(value - high, 8, 7).astype(BF16)


def three(value, axis):
    high, low = split(value)
    return jnp.concatenate([high, low, high], axis=axis)


def outer_three(value, axis):
    high, low = outer_split(value)
    return jnp.concatenate([high, high, low], axis=axis)


def dot(left, right, dims):
    return lax.dot_general(left, right, dims, preferred_element_type=F32)


def fields_of(scale, ctrls, perts, lat, lon, wrapped, out):
    nx = lon.shape[0]
    total = None
    for k in range(ctrls[0].shape[0]):
        ctrl = jnp.concatenate([p[k] for p in ctrls], axis=0)
        rowwise = dot(three(ctrl, 1), lon[...], NT)
        field = dot(lat[...], three(rowwise, 0), NN)
        product = jnp.concatenate([p[k] for p in perts], axis=0) * field
        total = product if total is None else total + product
    wrapped[8 : 8 + nx, :] = (total * scale).T
    wrapped[0:8, :] = wrapped[nx : nx + 8, :]
    wrapped[nx + 8 : nx + 16, :] = wrapped[8:16, :]
    windows, _, width, _ = out.shape
    step = nx // windows
    for m in range(windows):
        out[m, 0] = wrapped[step * m + 6 : step * m + 6 + width, :]


def overlapped(stripe, parts, out):
    windows, _, width, lats = out.shape
    total = None
    for s, part in enumerate(parts):
        window = part[...]
        grown = jnp.concatenate([window, jnp.zeros((width, lats - window.shape[1]), F32)], axis=1)
        turned = pltpu.roll(grown, (stripe * s - 2) % lats, 1)
        total = turned if total is None else total + turned
    for m in range(windows):
        out[m, out.shape[1] - 1] = total


def windows_of(stripe, parts, outs):
    total = parts[0, 0]
    for m in range(1, parts.shape[0]):
        total = total + parts[m, 0]
    lats = total.shape[1]
    for s, out in enumerate(outs):
        turned = pltpu.roll(total, (2 - stripe * s) % lats, 1)
        out[0] = turned[:, : out.shape[2]]


def adjoint_of(scale, grads, perts, lat, lon, wrapped, outs):
    stripe = perts[0].shape[1]
    nx = lon.shape[1]
    wrapped[...] = jnp.zeros_like(wrapped)
    windows, parts, width, _ = grads.shape
    step = nx // windows
    for m in range(windows):
        place = slice(step * m + 6, step * m + 6 + width)
        wrapped[place, :] = wrapped[place, :] + grads[m, parts - 1]
    wrapped[nx : nx + 8, :] = wrapped[nx : nx + 8, :] + wrapped[0:8, :]
    wrapped[8:16, :] = wrapped[8:16, :] + wrapped[nx + 8 : nx + 16, :]
    grad = wrapped[8 : 8 + nx, :].T * scale
    for k in range(perts[0].shape[0]):
        weighted = jnp.concatenate([p[k] for p in perts], axis=0) * grad
        half = dot(lat[...], three(weighted, 0), NN)
        result = dot(three(half, 1), lon[...], NN)
        for s, out in enumerate(outs):
            out[k] = result[stripe * s : stripe * (s + 1), :]


def fine_level(window, inn, weight, balance, rl3, ru3, rl_hi, rl_lo, rub3):
    nlat, nlon = inn.shape
    tall, wide = rl3.shape[0], ru3.shape[1]
    width = window.shape[0]
    win = three(window, 1)
    part = dot(rl3[...], jnp.concatenate([win] * 3, axis=0), NT)
    high = part.astype(BF16).astype(F32)
    lane = lax.broadcasted_iota(jnp.int32, part.shape, 1)
    part = jnp.where((lane >= width) & (lane < 2 * width), part - high, high).astype(BF16)
    field = dot(part, ru3[...], NN)
    centre = field[:, :nlon]
    image = (
        balance[0] * centre[:nlat]
        + balance[1] * pltpu.roll(field, wide - 1, 1)[:nlat, :nlon]
        + balance[2] * pltpu.roll(field, 1, 1)[:nlat, :nlon]
        + balance[3] * pltpu.roll(centre, tall - 1, 0)[:nlat]
        + balance[4] * pltpu.roll(centre, 1, 0)[:nlat]
    )
    misfit = weight * (image - inn)

    def longer(value):
        return jnp.concatenate([value, jnp.zeros((value.shape[0], wide - nlon), F32)], axis=1)

    def taller(value):
        return jnp.concatenate([value, jnp.zeros((tall - nlat, value.shape[1]), F32)], axis=0)

    across = (
        longer(balance[0] * misfit)
        + pltpu.roll(longer(balance[1] * misfit), 1, 1)
        + pltpu.roll(longer(balance[2] * misfit), wide - 1, 1)
    )
    along = pltpu.roll(taller(balance[3] * misfit), 1, 0) + pltpu.roll(taller(balance[4] * misfit), tall - 1, 0)
    grad = taller(across) + longer(along)
    back = dot(three(grad, 1), rub3[...], NT).T
    high, low = split(back)
    return dot(high, rl_hi[...], NN) + (dot(high, rl_lo[...], NN) + dot(low, rl_hi[...], NN))


def fine_kernel(bands, band_ref, *refs):
    wins, (inn, weight), consts = refs[:bands], refs[bands : bands + 2], refs[bands + 2 : bands + 8]
    outs, window = refs[bands + 8 : -1], refs[-1]
    turn, level = pl.program_id(0), pl.program_id(1)
    width = wins[0].shape[1]
    for s in range(bands):

        @pl.when(turn == s)
        def _():
            window[:width, :] = wins[s][level]

    if width < window.shape[0]:
        window[width:, :] = jnp.zeros((window.shape[0] - width, window.shape[1]), F32)
    result = fine_level(window[...], inn[0], weight[0], *consts)
    for s in range(bands):

        @pl.when(turn == s)
        def _():
            outs[s][level] = result[:width]


def add_kernel(bands, band_ref, ctrl, *refs):
    pieces, out = refs[:bands], refs[-1]
    band = band_ref[0]
    for s in range(bands):
        owner = lax.rem(band - s + bands, bands)
        out[0, owner, 0] = ctrl[0, owner, 0] + pieces[s][0, 0]


def scalar_grid(grid, in_specs, out_specs, scratch=()):
    return pltpu.PrefetchScalarGridSpec(
        num_scalar_prefetch=1, grid=grid, in_specs=in_specs, out_specs=out_specs, scratch_shapes=scratch
    )


def whole_block(array):
    return pl.BlockSpec(array.shape, lambda *ids: (0,) * len(array.shape))


def chunks_of(owned):
    count = math.gcd(owned, 4)
    return [(owned // count * i, owned // count) for i in range(count)]


def body(controls, members, loc_lon, loc_lat, balance, innovation, obs_weight):
    bands, mates = lax.axis_size("band"), lax.axis_size("member")
    band = lax.axis_index("band")
    band_array = jnp.reshape(band, (1,)).astype(jnp.int32)
    held, levels, cy, nx = controls.shape
    ny = loc_lat.shape[0]
    cx = nx // mates
    owned = levels // bands
    width, deep = round_up(cx + 4, 8), round_up(cx + 4, 16)
    lanes = min(round_up(cy + 4, 128), ny)
    nlat, nlon = innovation.shape[1:]
    tall, wide = nlat + 8, round_up(nlon + 2, 128)
    scale = 1.0 / math.sqrt(held * mates - 1)

    turned = jnp.roll(loc_lat, (-cy * band, -cy * band), (0, 1))
    lat3, lat_t3 = outer_three(turned, 1), outer_three(turned.T, 1)
    lon3, lon_b3 = outer_three(loc_lon, 1), outer_three(loc_lon, 0)
    ru = jnp.asarray(edged_matrix(cx, wide, deep).T)
    ru3, rub3 = outer_three(ru, 0), outer_three(ru, 1)
    row = lax.broadcasted_iota(jnp.int32, (tall, lanes), 0)
    col = lax.broadcasted_iota(jnp.int32, (tall, lanes), 1)
    first, last = band == 0, band == bands - 1
    off = (first & ((row == tall - 1) | (col < 2))) | (last & ((row == nlat) | (col >= cy + 2)))
    rl = jnp.where(off, 0.0, jnp.asarray(edged_matrix(cy, tall, lanes)))
    rl3, (rl_hi, rl_lo) = outer_three(rl, 1), outer_split(rl)

    plan = chunks_of(owned)
    count = plan[0][1]
    ctrl_view = controls.reshape(held, bands, owned, cy, nx)
    mem_view = members.reshape(held, bands, owned, cy, nx)
    wrap_scratch = pltpu.VMEM((nx + 16, ny), F32)

    def shifted(value, s):
        if s % bands == 0:
            return value
        return lax.ppermute(value, "band", [(i, (i + s) % bands) for i in range(bands)])

    def sent(views, first_level, s):
        at = lax.rem(band - s + bands, bands)
        size, start = (held, 1, count, cy, nx), (0, at, first_level, 0, 0)
        return jnp.stack([lax.dynamic_slice(v, start, size)[:, 0] for v in views])

    def received(views, first_level):
        return [shifted(sent(views, first_level, s), -s) for s in range(1, bands)]

    def own_spec(first_level):
        return pl.BlockSpec((held, None, None, cy, nx), lambda l, b: (0, b[0], first_level + l, 0, 0))

    def piece_spec(at):
        return pl.BlockSpec((None, held, None, cy, nx), lambda l, b: (at, 0, l, 0, 0))

    def swapped_spec(parts):
        return pl.BlockSpec((mates, parts, None, width, ny), lambda l, b: (0, 0, l, 0, 0))

    def small_spec(parts):
        return pl.BlockSpec((parts, None, width, lanes), lambda l, b: (0, l, 0, 0))

    def stage_in(first_level, pieces, coarse):
        arrays, specs = [], []
        if pieces is not None:
            for at, view in enumerate((ctrl_view, mem_view)):
                arrays += [view] + [p[0] for p in pieces[at]]
                specs += [own_spec(first_level)] + [piece_spec(p[1]) for p in pieces[at]]
            arrays += [lat3, lon3]
            specs += [whole_block(lat3), whole_block(lon3)]
        if coarse is not None:
            last = coarse[0].shape[0] - 1
            arrays += coarse
            specs += [pl.BlockSpec((None, None, width, lanes), lambda l, b: (last, l, 0, 0))] * bands
        parts = (pieces is not None) + (coarse is not None)

        def kernel(band_ref, *refs):
            refs = list(refs)
            wrapped, out = refs.pop(), refs.pop()
            if pieces is not None:
                fields_of(scale, refs[:bands], refs[bands : 2 * bands], *refs[2 * bands : 2 * bands + 2], wrapped, out)
            if coarse is not None:
                overlapped(cy, refs[-bands:], out)

        return pl.pallas_call(
            kernel,
            grid_spec=scalar_grid((count,), specs, swapped_spec(parts), [wrap_scratch]),
            out_shape=jax.ShapeDtypeStruct((mates, parts, count, width, ny), F32),
            name="stage_in",
        )(band_array, *arrays)

    def stage_out(swapped, fine_out):
        arrays, specs = [swapped], [swapped_spec(swapped.shape[1])]
        parts = 1 + (fine_out is not None)
        if fine_out is not None:
            arrays += fine_out
            specs += [pl.BlockSpec((None, None, width, lanes), lambda l, b: (0, l, 0, 0))] * bands

        def kernel(band_ref, *refs):
            outs = refs[len(arrays) :]
            windows_of(cy, refs[0], outs)
            if fine_out is not None:
                for s in range(bands):
                    outs[s][1] = refs[1 + (bands - s) % bands][...]

        return pl.pallas_call(
            kernel,
            grid_spec=scalar_grid((count,), specs, [small_spec(parts)] * bands),
            out_shape=[jax.ShapeDtypeStruct((parts, count, width, lanes), F32)] * bands,
            name="stage_out",
        )(band_array, *arrays)

    def adjoint(swapped, first_level, perts):
        arrays = [swapped, mem_view] + [p[0] for p in perts] + [lat_t3, lon_b3]
        specs = [swapped_spec(swapped.shape[1]), own_spec(first_level)] + [piece_spec(p[1]) for p in perts]
        specs += [whole_block(lat_t3), whole_block(lon_b3)]

        def kernel(band_ref, swap_ref, *refs):
            adjoint_of(scale, swap_ref, refs[:bands], *refs[bands : bands + 2], refs[-1], refs[bands + 2 : -1])

        return pl.pallas_call(
            kernel,
            grid_spec=scalar_grid(
                (count,),
                specs,
                [pl.BlockSpec((held, None, cy, nx), lambda l, b: (0, l, 0, 0))] * bands,
                [wrap_scratch],
            ),
            out_shape=[jax.ShapeDtypeStruct((held, count, cy, nx), F32)] * bands,
            name="adjoint",
        )(band_array, *arrays)

    def fine(wins, first_level):
        def level(o, l, b):
            return (lax.rem(b[0] - o + bands, bands) * owned + first_level + l, 0, 0)

        consts = (balance, rl3, ru3, rl_hi, rl_lo, rub3)
        return pl.pallas_call(
            functools.partial(fine_kernel, bands),
            grid_spec=scalar_grid(
                (bands, count),
                [pl.BlockSpec((None, count, width, lanes), lambda o, l, b: (0, 0, 0, 0))] * bands
                + [pl.BlockSpec((1, nlat, nlon), level)] * 2
                + [whole_block(c) for c in consts],
                [pl.BlockSpec((None, count, width, lanes), lambda o, l, b: (0, 0, 0, 0))] * bands,
                [pltpu.VMEM((deep, lanes), F32)],
            ),
            out_shape=[jax.ShapeDtypeStruct((1, count, width, lanes), F32)] * bands,
            name="fine",
        )(band_array, *wins, innovation, obs_weight, *consts)

    def added(result, pieces, first_level):
        block = pl.BlockSpec((1, bands, 1, cy, nx), lambda k, l, b: (k, 0, first_level + l, 0, 0))
        piece = pl.BlockSpec((1, 1, cy, nx), lambda k, l, b: (k, l, 0, 0))
        carried = [] if result is None else [result]
        return pl.pallas_call(
            functools.partial(add_kernel, bands),
            grid_spec=scalar_grid(
                (held, count),
                [block] + [piece] * bands + [pl.BlockSpec(memory_space=pl.ANY)] * len(carried),
                block,
            ),
            out_shape=jax.ShapeDtypeStruct(ctrl_view.shape, F32),
            input_output_aliases={2 + bands: 0} if carried else {},
            name="added",
        )(band_array, ctrl_view, *pieces, *carried)

    swap = functools.partial(lax.all_to_all, split_axis=0, concat_axis=0, tiled=True)
    total = len(plan)
    pieces, small, result = [], None, None
    for i, (first, _) in enumerate(plan):
        if i == 0:
            sides = []
            for view in (ctrl_view, mem_view):
                sides.append([(p, 0) for p in received((view,), first)])
        else:
            pair = received((ctrl_view, mem_view), first)
            sides = [[(p, 0) for p in pair], [(p, 1) for p in pair]]
        pieces.append(sides)
    for t in range(total + 2):
        now, middle, old = (i if 0 <= i < total else None for i in (t, t - 1, t - 2))
        level = None if now is None else plan[now][0]
        coarse = None if old is None else [small[(bands - s) % bands] for s in range(bands)]
        value = None
        if now is not None or old is not None:
            value = stage_in(level, None if now is None else pieces[now], coarse)
        if value is not None:
            value = swap(value, "member")
        fine_out = None
        if middle is not None:
            fine_out = fine(small, plan[middle][0])
        sending = None
        if now is not None:
            sending = stage_out(value, fine_out)
        elif fine_out is not None:
            sending = [fine_out[(bands - s) % bands] for s in range(bands)]
        if sending is not None:
            small = [shifted(p, s) for s, p in enumerate(sending)]
        if old is not None:
            back = adjoint(value, plan[old][0], pieces[old][1])
            back = [shifted(p, s) for s, p in enumerate(back)]
            result = added(result, back, plan[old][0])
    return result.reshape(controls.shape)


def solution(mesh):
    return jax.shard_map(
        body,
        mesh=mesh,
        in_specs=(
            P("member", None, "band", None),
            P("member", None, "band", None),
            P(),
            P(),
            P(None, "band", "member"),
            P(None, "band", "member"),
            P(None, "band", "member"),
        ),
        out_specs=P("member", None, "band", None),
        check_vma=False,
    )
```

profile of v0, /device:TPU:0, one launch (start us, length us, event | category | flops | bytes accessed | tf_op | source)
XLA Modules:
  0.0 393.0 jit_solution(17186388369053179439)
XLA Ops:
  3.4 5.1 %collective-permute-start.9 = (f32[1,2,1,64,512]{4,3,2,1,0:T(8,128)}, f32[1,2,1,64,512]{4,3,2,1,0:T(8,128)}, u32[]{:S(2)}, u32[]{:S(2)}) collective-permute-start(f32[1,2,1,64,512]{4,3,2,1,0:T(8,128)} %get-tuple-element.117), channel_id=1, source_target_pairs={{0,3},{1,0},{2,1},{3,2},{4,7},{5,4},{6,5},{7,6},{8,11},{9,8},{10,9... | collective-permute-start | bytes 786440 | tf_op jit(solution)/shard_map/ppermute | solution.py:244
  18.0 8.1 %collective-permute-start.14 = (f32[1,2,1,64,512]{4,3,2,1,0:T(8,128)}, f32[1,2,1,64,512]{4,3,2,1,0:T(8,128)S(1)}, u32[]{:S(2)}, u32[]{:S(2)}) collective-permute-start(f32[1,2,1,64,512]{4,3,2,1,0:T(8,128)} %get-tuple-element.103), channel_id=1, source_target_pairs={{0,1},{1,2},{2,3},{3,0},{4,5},{5,6},{6,7},{7,4},{8,9},{9,10},{10,1... | collective-permute-start | bytes 786440 | tf_op jit(solution)/shard_map/ppermute | solution.py:244
  27.8 5.6 %collective-permute-done.10.refs_2_ = f32[1,2,1,64,512]{4,3,2,1,0:T(8,128)} collective-permute-done((f32[1,2,1,64,512]{4,3,2,1,0:T(8,128)}, f32[1,2,1,64,512]{4,3,2,1,0:T(8,128)}, u32[]{:S(2)}, u32[]{:S(2)}) %collective-permute-start.10) | collective-permute-done | bytes 262176 | tf_op jit(solution)/shard_map/ppermute | solution.py:244
  33.4 13.7 %collective-permute-start.7 = (f32[2,2,1,64,512]{4,3,2,1,0:T(8,128)}, f32[2,2,1,64,512]{4,3,2,1,0:T(8,128)S(1)}, u32[]{:S(2)}, u32[]{:S(2)}) collective-permute-start(f32[2,2,1,64,512]{4,3,2,1,0:T(8,128)} %pad_maximum_fusion.9), channel_id=1, source_target_pairs={{0,2},{1,3},{2,0},{3,1},{4,6},{5,7},{6,4},{7,5},{8,10},{9,11},{10,... | collective-permute-start | bytes 1572872 | tf_op jit(solution)/shard_map/ppermute | solution.py:244
  50.5 5.3 %collective-permute-done.13.refs_6_.refs_2_ = f32[1,2,1,64,512]{4,3,2,1,0:T(8,128)S(1)} collective-permute-done((f32[1,2,1,64,512]{4,3,2,1,0:T(8,128)}, f32[1,2,1,64,512]{4,3,2,1,0:T(8,128)S(1)}, u32[]{:S(2)}, u32[]{:S(2)}) %collective-permute-start.13) | collective-permute-done | bytes 262176 | tf_op jit(solution)/shard_map/ppermute | solution.py:244
  56.6 4.9 %stage_in.7 = f32[8,1,1,72,256]{4,3,2,1,0:T(8,128)} custom-call(s32[1]{0:T(128)} %bitcast.band_ref, f32[2,4,4,64,512]{4,3,2,1,0:T(8,128)} %bitcast.65, f32[1,2,1,64,512]{4,3,2,1,0:T(8,128)} %collective-permute-done.9.refs_1_, f32[1,2,1,64,512]{4,3,2,1,0:T(8,128)} %collective-permute-done.10.refs_2_, f32[1,2,1,64,512]{4,3,2,1,0:T(8,128)} %collective-permute-done.11.refs_3_, ...), custom_call_target="tpu_custom_call" | custom-call | tf_op jit(solution)/shard_map/stage_in/pallas_call | solution.py:288
  67.6 19.1 %collective-permute-start.3 = (f32[2,2,1,64,512]{4,3,2,1,0:T(8,128)}, f32[2,2,1,64,512]{4,3,2,1,0:T(8,128)S(1)}, u32[]{:S(2)}, u32[]{:S(2)}) collective-permute-start(f32[2,2,1,64,512]{4,3,2,1,0:T(8,128)} %pad_maximum_fusion.5), channel_id=1, source_target_pairs={{0,3},{1,0},{2,1},{3,2},{4,7},{5,4},{6,5},{7,6},{8,11},{9,8},{10,9... | collective-permute-start | bytes 1572872 | tf_op jit(solution)/shard_map/ppermute | solution.py:244
  101.2 4.8 %stage_in.6 = f32[8,1,1,72,256]{4,3,2,1,0:T(8,128)} custom-call(s32[1]{0:T(128)} %bitcast.band_ref, f32[2,4,4,64,512]{4,3,2,1,0:T(8,128)} %bitcast.66, f32[2,2,1,64,512]{4,3,2,1,0:T(8,128)} %copy-done.3, f32[2,2,1,64,512]{4,3,2,1,0:T(8,128)} %copy-done.4, f32[2,2,1,64,512]{4,3,2,1,0:T(8,128)} %copy-done.5, f32[2,4,4,64,512]{4,3,2,1,0:T(8,128)} %bitcast.56, ...), custom_call_target="tpu_custom_call" | custom-call | tf_op jit(solution)/shard_map/stage_in/pallas_call | solution.py:288
  111.7 22.4 %collective-permute-start.15 = (f32[1,1,72,128]{3,2,1,0:T(8,128)}, f32[1,1,72,128]{3,2,1,0:T(8,128)S(1)}, u32[]{:S(2)}, u32[]{:S(2)}) collective-permute-start(f32[1,1,72,128]{3,2,1,0:T(8,128)} %get-tuple-element.54), channel_id=1, source_target_pairs={{0,1},{1,2},{2,3},{3,0},{4,5},{5,6},{6,7},{7,4},{8,9},{9,10},{10,1... | collective-permute-start | bytes 110600 | tf_op jit(solution)/shard_map/ppermute | solution.py:244
  140.6 5.2 %collective-permute-done.16.refs_2_ = f32[1,1,72,128]{3,2,1,0:T(8,128)S(1)} collective-permute-done((f32[1,1,72,128]{3,2,1,0:T(8,128)}, f32[1,1,72,128]{3,2,1,0:T(8,128)S(1)}, u32[]{:S(2)}, u32[]{:S(2)}) %collective-permute-start.16) | collective-permute-done | bytes 36896 | tf_op jit(solution)/shard_map/ppermute | solution.py:244
  150.0 8.9 %fine.4 = (f32[1,1,72,128]{3,2,1,0:T(8,128)}, f32[1,1,72,128]{3,2,1,0:T(8,128)}, f32[1,1,72,128]{3,2,1,0:T(8,128)}, f32[1,1,72,128]{3,2,1,0:T(8,128)}) custom-call(s32[1]{0:T(128)} %bitcast.band_ref, f32[1,1,72,128]{3,2,1,0:T(8,128)} %get-tuple-element.53.refs_0_, f32[1,1,72,128]{3,2,1,0:T(8,128)} %copy-done.57, f32[1,1,72,128]{3,2,1,0:T(8,128)} %copy-done.58, ...), custom_call_target="tpu_custom_call" | custom-call | tf_op jit(solution)/shard_map/fine/pallas_call | solution.py:341
  172.5 5.0 %stage_in.8 = f32[8,2,1,72,256]{4,3,2,1,0:T(8,128)} custom-call(s32[1]{0:T(128)} %bitcast.band_ref, f32[2,4,4,64,512]{4,3,2,1,0:T(8,128)} %bitcast.67, f32[2,2,1,64,512]{4,3,2,1,0:T(8,128)} %copy-done.6, f32[2,2,1,64,512]{4,3,2,1,0:T(8,128)} %copy-done.7, f32[2,2,1,64,512]{4,3,2,1,0:T(8,128)} %copy-done.8, f32[2,4,4,64,512]{4,3,2,1,0:T(8,128)} %bitcast.57, ...), custom_call_target="tpu_custom_call" | custom-call | tf_op jit(solution)/shard_map/stage_in/pallas_call | solution.py:288
  187.9 8.9 %fine.5 = (f32[1,1,72,128]{3,2,1,0:T(8,128)}, f32[1,1,72,128]{3,2,1,0:T(8,128)}, f32[1,1,72,128]{3,2,1,0:T(8,128)}, f32[1,1,72,128]{3,2,1,0:T(8,128)}) custom-call(s32[1]{0:T(128)} %bitcast.band_ref, f32[2,1,72,128]{3,2,1,0:T(8,128)} %get-tuple-element.61.refs_10_.refs_0_, f32[2,1,72,128]{3,2,1,0:T(8,128)} %copy-done.37, f32[2,1,72,128]{3,2,1,0:T(8,128)} %copy-done.36, ...), custom_call_target="tpu_custom_call" | custom-call | tf_op jit(solution)/shard_map/fine/pallas_call | solution.py:341
  204.3 30.5 %collective-permute-done.1.refs_2_.refs_6_ = f32[2,2,1,64,512]{4,3,2,1,0:T(8,128)S(1)} collective-permute-done((f32[2,2,1,64,512]{4,3,2,1,0:T(8,128)}, f32[2,2,1,64,512]{4,3,2,1,0:T(8,128)S(1)}, u32[]{:S(2)}, u32[]{:S(2)}) %collective-permute-start.1) | collective-permute-done | bytes 524320 | tf_op jit(solution)/shard_map/ppermute | solution.py:244
  238.1 5.0 %stage_in.9 = f32[8,2,1,72,256]{4,3,2,1,0:T(8,128)} custom-call(s32[1]{0:T(128)} %bitcast.band_ref, f32[2,4,4,64,512]{4,3,2,1,0:T(8,128)} %bitcast.68, f32[2,2,1,64,512]{4,3,2,1,0:T(8,128)} %copy-done.9, f32[2,2,1,64,512]{4,3,2,1,0:T(8,128)} %copy-done.10, f32[2,2,1,64,512]{4,3,2,1,0:T(8,128)} %copy-done.11, f32[2,4,4,64,512]{4,3,2,1,0:T(8,128)} %bitcast.58, ...), custom_call_target="tpu_custom_call" | custom-call | tf_op jit(solution)/shard_map/stage_in/pallas_call | solution.py:288
  246.9 8.9 %fine.6 = (f32[1,1,72,128]{3,2,1,0:T(8,128)}, f32[1,1,72,128]{3,2,1,0:T(8,128)}, f32[1,1,72,128]{3,2,1,0:T(8,128)}, f32[1,1,72,128]{3,2,1,0:T(8,128)}) custom-call(s32[1]{0:T(128)} %bitcast.band_ref, f32[2,1,72,128]{3,2,1,0:T(8,128)} %get-tuple-element.69.refs_10_.refs_0_, f32[2,1,72,128]{3,2,1,0:T(8,128)} %copy-done.40, f32[2,1,72,128]{3,2,1,0:T(8,128)} %copy-done.39, ...), custom_call_target="tpu_custom_call" | custom-call | tf_op jit(solution)/shard_map/fine/pallas_call | solution.py:341
  255.8 7.8 %all-to-all-done.3.refs_0_.swap_ref = f32[8,2,1,72,256]{4,3,2,1,0:T(8,128)S(1)} async-done(((f32[8,2,1,72,256]{4,3,2,1,0:T(8,128)}), f32[8,2,1,72,256]{4,3,2,1,0:T(8,128)S(1)}, u32[]{:S(2)}, u32[]{:S(2)}) %all-to-all-start.3) | async-done | bytes 1179680 | tf_op jit(solution)/shard_map/all_to_all | solution.py:391
  281.9 8.9 %fine.7 = (f32[1,1,72,128]{3,2,1,0:T(8,128)}, f32[1,1,72,128]{3,2,1,0:T(8,128)}, f32[1,1,72,128]{3,2,1,0:T(8,128)}, f32[1,1,72,128]{3,2,1,0:T(8,128)}) custom-call(s32[1]{0:T(128)} %bitcast.band_ref, f32[2,1,72,128]{3,2,1,0:T(8,128)} %get-tuple-element.77.refs_0_, f32[2,1,72,128]{3,2,1,0:T(8,128)} %copy-done.41, f32[2,1,72,128]{3,2,1,0:T(8,128)} %copy-done.42, ...), custom_call_target="tpu_custom_call" | custom-call | tf_op jit(solution)/shard_map/fine/pallas_call | solution.py:341
  296.1 4.8 %adjoint.7 = (f32[2,1,64,512]{3,2,1,0:T(8,128)}, f32[2,1,64,512]{3,2,1,0:T(8,128)}, f32[2,1,64,512]{3,2,1,0:T(8,128)}, f32[2,1,64,512]{3,2,1,0:T(8,128)}) custom-call(s32[1]{0:T(128)} %bitcast.band_ref, f32[8,2,1,72,256]{4,3,2,1,0:T(8,128)} %copy-done.2, f32[2,4,4,64,512]{4,3,2,1,0:T(8,128)} %bitcast.59, f32[1,2,1,64,512]{4,3,2,1,0:T(8,128)} %copy-done.21, ...), custom_call_target="tpu_custom_call" | custom-call | tf_op jit(solution)/shard_map/adjoint/pallas_call | solution.py:324
  334.0 5.3 %collective-permute-start.34 = (f32[2,1,64,512]{3,2,1,0:T(8,128)}, f32[2,1,64,512]{3,2,1,0:T(8,128)S(1)}, u32[]{:S(2)}, u32[]{:S(2)}) collective-permute-start(f32[2,1,64,512]{3,2,1,0:T(8,128)} %get-tuple-element.91), channel_id=1, source_target_pairs={{0,2},{1,3},{2,0},{3,1},{4,6},{5,7},{6,4},{7,5},{8,10},{9,11},{10,... | collective-permute-start | bytes 786440 | tf_op jit(solution)/shard_map/ppermute | solution.py:244
  343.0 13.1 %collective-permute-done.37.refs_2_ = f32[2,1,64,512]{3,2,1,0:T(8,128)S(1)} collective-permute-done((f32[2,1,64,512]{3,2,1,0:T(8,128)}, f32[2,1,64,512]{3,2,1,0:T(8,128)S(1)}, u32[]{:S(2)}, u32[]{:S(2)}) %collective-permute-start.37) | collective-permute-done | bytes 262176 | tf_op jit(solution)/shard_map/ppermute | solution.py:244
  356.1 5.3 %collective-permute-start.30 = (f32[2,1,64,512]{3,2,1,0:T(8,128)}, f32[2,1,64,512]{3,2,1,0:T(8,128)S(1)}, u32[]{:S(2)}, u32[]{:S(2)}) collective-permute-start(f32[2,1,64,512]{3,2,1,0:T(8,128)} %get-tuple-element.86), channel_id=1, source_target_pairs={{0,1},{1,2},{2,3},{3,0},{4,5},{5,6},{6,7},{7,4},{8,9},{9,10},{10,1... | collective-permute-start | bytes 786440 | tf_op jit(solution)/shard_map/ppermute | solution.py:244
  369.6 9.0 %collective-permute-done.34.refs_2_ = f32[2,1,64,512]{3,2,1,0:T(8,128)S(1)} collective-permute-done((f32[2,1,64,512]{3,2,1,0:T(8,128)}, f32[2,1,64,512]{3,2,1,0:T(8,128)S(1)}, u32[]{:S(2)}, u32[]{:S(2)}) %collective-permute-start.34) | collective-permute-done | bytes 262176 | tf_op jit(solution)/shard_map/ppermute | solution.py:244
  381.7 8.1 %collective-permute-done.31.refs_2_ = f32[2,1,64,512]{3,2,1,0:T(8,128)S(1)} collective-permute-done((f32[2,1,64,512]{3,2,1,0:T(8,128)}, f32[2,1,64,512]{3,2,1,0:T(8,128)S(1)}, u32[]{:S(2)}, u32[]{:S(2)}) %collective-permute-start.31) | collective-permute-done | bytes 262176 | tf_op jit(solution)/shard_map/ppermute | solution.py:244
  (250 shorter events, 168.7 us)
Async XLA Ops:
  11.3 35.9 %collective-permute-start.12 = (f32[1,2,1,64,512]{4,3,2,1,0:T(8,128)}, f32[1,2,1,64,512]{4,3,2,1,0:T(8,128)S(1)}, u32[]{:S(2)}, u32[]{:S(2)}) collective-permute-start(f32[1,2,1,64,512]{4,3,2,1,0:T(8,128)} %get-tuple-element.105), channel_id=1, source_target_pairs={{0,3},{1,0},{2,1},{3,2},{4,7},{5,4},{6,5},{7,6},{8,11},{9,8},{10,9... | collective-permute-start | bytes 786440 | tf_op jit(solution)/shard_map/ppermute | solution.py:244
  14.1 41.7 %collective-permute-start.13 = (f32[1,2,1,64,512]{4,3,2,1,0:T(8,128)}, f32[1,2,1,64,512]{4,3,2,1,0:T(8,128)S(1)}, u32[]{:S(2)}, u32[]{:S(2)}) collective-permute-start(f32[1,2,1,64,512]{4,3,2,1,0:T(8,128)} %get-tuple-element.104), channel_id=1, source_target_pairs={{0,2},{1,3},{2,0},{3,1},{4,6},{5,7},{6,4},{7,5},{8,10},{9,11},{10,... | collective-permute-start | bytes 786440 | tf_op jit(solution)/shard_map/ppermute | solution.py:244
  18.0 37.8 %collective-permute-start.14 = (f32[1,2,1,64,512]{4,3,2,1,0:T(8,128)}, f32[1,2,1,64,512]{4,3,2,1,0:T(8,128)S(1)}, u32[]{:S(2)}, u32[]{:S(2)}) collective-permute-start(f32[1,2,1,64,512]{4,3,2,1,0:T(8,128)} %get-tuple-element.103), channel_id=1, source_target_pairs={{0,1},{1,2},{2,3},{3,0},{4,5},{5,6},{6,7},{7,4},{8,9},{9,10},{10,1... | collective-permute-start | bytes 786440 | tf_op jit(solution)/shard_map/ppermute | solution.py:244
  33.4 61.7 %collective-permute-start.6 = (f32[2,2,1,64,512]{4,3,2,1,0:T(8,128)}, f32[2,2,1,64,512]{4,3,2,1,0:T(8,128)S(1)}, u32[]{:S(2)}, u32[]{:S(2)}) collective-permute-start(f32[2,2,1,64,512]{4,3,2,1,0:T(8,128)} %pad_maximum_fusion.8), channel_id=1, source_target_pairs={{0,3},{1,0},{2,1},{3,2},{4,7},{5,4},{6,5},{7,6},{8,11},{9,8},{10,9... | collective-permute-start | bytes 1572872 | tf_op jit(solution)/shard_map/ppermute | solution.py:244
  33.4 66.2 %collective-permute-start.7 = (f32[2,2,1,64,512]{4,3,2,1,0:T(8,128)}, f32[2,2,1,64,512]{4,3,2,1,0:T(8,128)S(1)}, u32[]{:S(2)}, u32[]{:S(2)}) collective-permute-start(f32[2,2,1,64,512]{4,3,2,1,0:T(8,128)} %pad_maximum_fusion.9), channel_id=1, source_target_pairs={{0,2},{1,3},{2,0},{3,1},{4,6},{5,7},{6,4},{7,5},{8,10},{9,11},{10,... | collective-permute-start | bytes 1572872 | tf_op jit(solution)/shard_map/ppermute | solution.py:244
  47.1 52.5 %collective-permute-start.8 = (f32[2,2,1,64,512]{4,3,2,1,0:T(8,128)}, f32[2,2,1,64,512]{4,3,2,1,0:T(8,128)S(1)}, u32[]{:S(2)}, u32[]{:S(2)}) collective-permute-start(f32[2,2,1,64,512]{4,3,2,1,0:T(8,128)} %pad_maximum_fusion.10), channel_id=1, source_target_pairs={{0,1},{1,2},{2,3},{3,0},{4,5},{5,6},{6,7},{7,4},{8,9},{9,10},{10,1... | collective-permute-start | bytes 1572872 | tf_op jit(solution)/shard_map/ppermute | solution.py:244
  61.5 44.6 %all-to-all-start.1 = ((f32[8,1,1,72,256]{4,3,2,1,0:T(8,128)}), f32[8,1,1,72,256]{4,3,2,1,0:T(8,128)}, u32[]{:S(2)}, u32[]{:S(2)}) async-start(f32[8,1,1,72,256]{4,3,2,1,0:T(8,128)} %stage_in.7), calls=%async_computation.1 | async-start | bytes 1179648 | tf_op jit(solution)/shard_map/all_to_all | solution.py:391
  67.6 97.9 %collective-permute-start.3 = (f32[2,2,1,64,512]{4,3,2,1,0:T(8,128)}, f32[2,2,1,64,512]{4,3,2,1,0:T(8,128)S(1)}, u32[]{:S(2)}, u32[]{:S(2)}) collective-permute-start(f32[2,2,1,64,512]{4,3,2,1,0:T(8,128)} %pad_maximum_fusion.5), channel_id=1, source_target_pairs={{0,3},{1,0},{2,1},{3,2},{4,7},{5,4},{6,5},{7,6},{8,11},{9,8},{10,9... | collective-permute-start | bytes 1572872 | tf_op jit(solution)/shard_map/ppermute | solution.py:244
  88.5 79.0 %collective-permute-start.4 = (f32[2,2,1,64,512]{4,3,2,1,0:T(8,128)}, f32[2,2,1,64,512]{4,3,2,1,0:T(8,128)S(1)}, u32[]{:S(2)}, u32[]{:S(2)}) collective-permute-start(f32[2,2,1,64,512]{4,3,2,1,0:T(8,128)} %pad_maximum_fusion.6), channel_id=1, source_target_pairs={{0,2},{1,3},{2,0},{3,1},{4,6},{5,7},{6,4},{7,5},{8,10},{9,11},{10,... | collective-permute-start | bytes 1572872 | tf_op jit(solution)/shard_map/ppermute | solution.py:244
  95.1 72.4 %collective-permute-start.5 = (f32[2,2,1,64,512]{4,3,2,1,0:T(8,128)}, f32[2,2,1,64,512]{4,3,2,1,0:T(8,128)S(1)}, u32[]{:S(2)}, u32[]{:S(2)}) collective-permute-start(f32[2,2,1,64,512]{4,3,2,1,0:T(8,128)} %pad_maximum_fusion.7), channel_id=1, source_target_pairs={{0,1},{1,2},{2,3},{3,0},{4,5},{5,6},{6,7},{7,4},{8,9},{9,10},{10,1... | collective-permute-start | bytes 1572872 | tf_op jit(solution)/shard_map/ppermute | solution.py:244
  106.1 52.8 %all-to-all-start = ((f32[8,1,1,72,256]{4,3,2,1,0:T(8,128)}), f32[8,1,1,72,256]{4,3,2,1,0:T(8,128)S(1)}, u32[]{:S(2)}, u32[]{:S(2)}) async-start(f32[8,1,1,72,256]{4,3,2,1,0:T(8,128)} %stage_in.6), calls=%async_computation | async-start | bytes 1179648 | tf_op jit(solution)/shard_map/all_to_all | solution.py:391
  185.1 49.6 %collective-permute-start.1 = (f32[2,2,1,64,512]{4,3,2,1,0:T(8,128)}, f32[2,2,1,64,512]{4,3,2,1,0:T(8,128)S(1)}, u32[]{:S(2)}, u32[]{:S(2)}) collective-permute-start(f32[2,2,1,64,512]{4,3,2,1,0:T(8,128)} %pad_maximum_fusion.3), channel_id=1, source_target_pairs={{0,2},{1,3},{2,0},{3,1},{4,6},{5,7},{6,4},{7,5},{8,10},{9,11},{10,... | collective-permute-start | bytes 1572872 | tf_op jit(solution)/shard_map/ppermute | solution.py:244
  186.6 48.2 %collective-permute-start.2 = (f32[2,2,1,64,512]{4,3,2,1,0:T(8,128)}, f32[2,2,1,64,512]{4,3,2,1,0:T(8,128)S(1)}, u32[]{:S(2)}, u32[]{:S(2)}) collective-permute-start(f32[2,2,1,64,512]{4,3,2,1,0:T(8,128)} %pad_maximum_fusion.4), channel_id=1, source_target_pairs={{0,1},{1,2},{2,3},{3,0},{4,5},{5,6},{6,7},{7,4},{8,9},{9,10},{10,1... | collective-permute-start | bytes 1572872 | tf_op jit(solution)/shard_map/ppermute | solution.py:244
  201.3 33.4 %collective-permute-start.21 = (f32[2,1,72,128]{3,2,1,0:T(8,128)}, f32[2,1,72,128]{3,2,1,0:T(8,128)S(1)}, u32[]{:S(2)}, u32[]{:S(2)}) collective-permute-start(f32[2,1,72,128]{3,2,1,0:T(8,128)} %get-tuple-element.70), channel_id=1, source_target_pairs={{0,3},{1,0},{2,1},{3,2},{4,7},{5,4},{6,5},{7,6},{8,11},{9,8},{10,9... | collective-permute-start | bytes 221192 | tf_op jit(solution)/shard_map/ppermute | solution.py:244
  202.5 35.0 %collective-permute-start.22 = (f32[2,1,72,128]{3,2,1,0:T(8,128)}, f32[2,1,72,128]{3,2,1,0:T(8,128)S(1)}, u32[]{:S(2)}, u32[]{:S(2)}) collective-permute-start(f32[2,1,72,128]{3,2,1,0:T(8,128)} %get-tuple-element.71), channel_id=1, source_target_pairs={{0,2},{1,3},{2,0},{3,1},{4,6},{5,7},{6,4},{7,5},{8,10},{9,11},{10,... | collective-permute-start | bytes 221192 | tf_op jit(solution)/shard_map/ppermute | solution.py:244
  203.0 34.4 %collective-permute-start.23 = (f32[2,1,72,128]{3,2,1,0:T(8,128)}, f32[2,1,72,128]{3,2,1,0:T(8,128)S(1)}, u32[]{:S(2)}, u32[]{:S(2)}) collective-permute-start(f32[2,1,72,128]{3,2,1,0:T(8,128)} %get-tuple-element.72), channel_id=1, source_target_pairs={{0,1},{1,2},{2,3},{3,0},{4,5},{5,6},{6,7},{7,4},{8,9},{9,10},{10,1... | collective-permute-start | bytes 221192 | tf_op jit(solution)/shard_map/ppermute | solution.py:244
  276.9 30.3 %all-to-all-start.5 = ((f32[8,1,1,72,256]{4,3,2,1,0:T(8,128)}), f32[8,1,1,72,256]{4,3,2,1,0:T(8,128)S(1)}, u32[]{:S(2)}, u32[]{:S(2)}) async-start(f32[8,1,1,72,256]{4,3,2,1,0:T(8,128)} %stage_in.11), calls=%async_computation.5 | async-start | bytes 1179648 | tf_op jit(solution)/shard_map/all_to_all | solution.py:391
  318.1 38.0 %collective-permute-start.37 = (f32[2,1,64,512]{3,2,1,0:T(8,128)}, f32[2,1,64,512]{3,2,1,0:T(8,128)S(1)}, u32[]{:S(2)}, u32[]{:S(2)}) collective-permute-start(f32[2,1,64,512]{3,2,1,0:T(8,128)} %get-tuple-element.95), channel_id=1, source_target_pairs={{0,2},{1,3},{2,0},{3,1},{4,6},{5,7},{6,4},{7,5},{8,10},{9,11},{10,... | collective-permute-start | bytes 786440 | tf_op jit(solution)/shard_map/ppermute | solution.py:244
  324.8 36.7 %collective-permute-start.38 = (f32[2,1,64,512]{3,2,1,0:T(8,128)S(1)}, f32[2,1,64,512]{3,2,1,0:T(8,128)S(1)}, u32[]{:S(2)}, u32[]{:S(2)}) collective-permute-start(f32[2,1,64,512]{3,2,1,0:T(8,128)S(1)} %copy-done.64), channel_id=1, source_target_pairs={{0,3},{1,0},{2,1},{3,2},{4,7},{5,4},{6,5},{7,6},{8,11},{9,8},{10,9... | collective-permute-start | bytes 786440 | tf_op jit(solution)/shard_map/ppermute | solution.py:244
  326.1 38.6 %collective-permute-start.33 = (f32[2,1,64,512]{3,2,1,0:T(8,128)}, f32[2,1,64,512]{3,2,1,0:T(8,128)S(1)}, u32[]{:S(2)}, u32[]{:S(2)}) collective-permute-start(f32[2,1,64,512]{3,2,1,0:T(8,128)} %get-tuple-element.90), channel_id=1, source_target_pairs={{0,1},{1,2},{2,3},{3,0},{4,5},{5,6},{6,7},{7,4},{8,9},{9,10},{10,1... | collective-permute-start | bytes 786440 | tf_op jit(solution)/shard_map/ppermute | solution.py:244
  334.0 44.6 %collective-permute-start.34 = (f32[2,1,64,512]{3,2,1,0:T(8,128)}, f32[2,1,64,512]{3,2,1,0:T(8,128)S(1)}, u32[]{:S(2)}, u32[]{:S(2)}) collective-permute-start(f32[2,1,64,512]{3,2,1,0:T(8,128)} %get-tuple-element.91), channel_id=1, source_target_pairs={{0,2},{1,3},{2,0},{3,1},{4,6},{5,7},{6,4},{7,5},{8,10},{9,11},{10,... | collective-permute-start | bytes 786440 | tf_op jit(solution)/shard_map/ppermute | solution.py:244
  339.3 39.3 %collective-permute-start.35 = (f32[2,1,64,512]{3,2,1,0:T(8,128)S(1)}, f32[2,1,64,512]{3,2,1,0:T(8,128)S(1)}, u32[]{:S(2)}, u32[]{:S(2)}) collective-permute-start(f32[2,1,64,512]{3,2,1,0:T(8,128)S(1)} %copy-done.63), channel_id=1, source_target_pairs={{0,3},{1,0},{2,1},{3,2},{4,7},{5,4},{6,5},{7,6},{8,11},{9,8},{10,9... | collective-permute-start | bytes 786440 | tf_op jit(solution)/shard_map/ppermute | solution.py:244
  356.1 25.6 %collective-permute-start.30 = (f32[2,1,64,512]{3,2,1,0:T(8,128)}, f32[2,1,64,512]{3,2,1,0:T(8,128)S(1)}, u32[]{:S(2)}, u32[]{:S(2)}) collective-permute-start(f32[2,1,64,512]{3,2,1,0:T(8,128)} %get-tuple-element.86), channel_id=1, source_target_pairs={{0,1},{1,2},{2,3},{3,0},{4,5},{5,6},{6,7},{7,4},{8,9},{9,10},{10,1... | collective-permute-start | bytes 786440 | tf_op jit(solution)/shard_map/ppermute | solution.py:244
  361.4 28.4 %collective-permute-start.31 = (f32[2,1,64,512]{3,2,1,0:T(8,128)}, f32[2,1,64,512]{3,2,1,0:T(8,128)S(1)}, u32[]{:S(2)}, u32[]{:S(2)}) collective-permute-start(f32[2,1,64,512]{3,2,1,0:T(8,128)} %get-tuple-element.87), channel_id=1, source_target_pairs={{0,2},{1,3},{2,0},{3,1},{4,6},{5,7},{6,4},{7,5},{8,10},{9,11},{10,... | collective-permute-start | bytes 786440 | tf_op jit(solution)/shard_map/ppermute | solution.py:244
  (89 other events, 933.0 us)
where the time goes:
time: 398 us; the launch traced here: 393 us
  starting transfers between devices  162 us (41%)
  waiting for transfers between devices  101 us (25%)
  Pallas kernels  95.2 us (24%)
  other arithmetic  17.1 us (4%)
  local copies, waits for them, and re-layouts  17 us (4%)
    ppermute x42, starting transfers between devices, shifted(): lax.ppermute(value, 'band', [(i, (i + s) % bands) for i in range(bands)])  138 us
    ppermute x42, waiting for transfers between devices, shifted(): lax.ppermute(value, 'band', [(i, (i + s) % bands) for i in range(bands)])  92.2 us
    pallas_call x4, Pallas kernels, fine(): pl.pallas_call(functools.partial(fine_kernel, bands), grid_spec=scalar_gr...  35.6 us
    all_to_all x6, starting transfers between devices, body(): value = swap(value, 'member')  23.6 us
    pallas_call x6, Pallas kernels, stage_in(): pl.pallas_call(kernel, grid_spec=scalar_grid((count,), specs, swapped_spe...  23.3 us
    pallas_call x4, Pallas kernels, adjoint(): pl.pallas_call(kernel, grid_spec=scalar_grid((count,), specs, [pl.BlockSp...  18.8 us
    another operation x9, other arithmetic, sent(): return jnp.stack([lax.dynamic_slice(v, start, size)[:, 0] for v in views])  11.5 us
    unnamed x131, local copies, waits for them, and re-layouts  10.9 us
  transfers between devices with their start and end apart: 48, of which 17 were waited for; matrix products, arithmetic and copies ran while one was open for 5% of the time, Pallas kernels for 20%

commit v1 on v0

--- a/solution.py
+++ b/solution.py
@@ -64,14 +64,17 @@
     return lax.dot_general(left, right, dims, preferred_element_type=F32)
 
 
-def fields_of(scale, ctrls, perts, lat, lon, wrapped, out):
-    nx = lon.shape[0]
+def field_of(ctrls, lat, lon, k):
+    ctrl = jnp.concatenate([p[k] for p in ctrls], axis=0)
+    rowwise = dot(three(ctrl, 1), lon[...], NT)
+    return dot(lat[...], three(rowwise, 0), NN)
+
+
+def increment_of(scale, field, perts, wrapped, out):
+    nx = wrapped.shape[0] - 16
     total = None
-    for k in range(ctrls[0].shape[0]):
-        ctrl = jnp.concatenate([p[k] for p in ctrls], axis=0)
-        rowwise = dot(three(ctrl, 1), lon[...], NT)
-        field = dot(lat[...], three(rowwise, 0), NN)
-        product = jnp.concatenate([p[k] for p in perts], axis=0) * field
+    for k in range(perts[0].shape[0]):
+        product = jnp.concatenate([p[k] for p in perts], axis=0) * field(k)
         total = product if total is None else total + product
     wrapped[8 : 8 + nx, :] = (total * scale).T
     wrapped[0:8, :] = wrapped[nx : nx + 8, :]
@@ -86,7 +89,7 @@
     windows, _, width, lats = out.shape
     total = None
     for s, part in enumerate(parts):
-        window = part[...]
+        window = part[...] if part.shape[0] == width else unpacked(stripe, part[...], True)
         grown = jnp.concatenate([window, jnp.zeros((width, lats - window.shape[1]), F32)], axis=1)
         turned = pltpu.roll(grown, (stripe * s - 2) % lats, 1)
         total = turned if total is None else total + turned
@@ -94,14 +97,31 @@
         out[m, out.shape[1] - 1] = total
 
 
-def windows_of(stripe, parts, outs):
+def packed(stripe, window, result):
+    lanes = window.shape[1]
+    lane = lax.broadcasted_iota(jnp.int32, window.shape, 1)
+    low = jnp.where(lane < stripe, window, pltpu.roll(result, stripe, 1))
+    edge = jnp.where(lane < stripe + 4, window, pltpu.roll(result, 4, 1))
+    edge = jnp.concatenate([edge, jnp.zeros((lanes - edge.shape[0], lanes), F32)], axis=0)
+    return jnp.concatenate([low, edge.T[stripe : stripe + 8]], axis=0)
+
+
+def unpacked(stripe, value, second):
+    width, lanes = value.shape[0] - 8, value.shape[1]
+    low, edge = value[:width], value[width:]
+    edge = jnp.concatenate([edge, jnp.zeros((lanes - 8, lanes), F32)], axis=0).T[:width]
+    lane = lax.broadcasted_iota(jnp.int32, low.shape, 1)
+    if second:
+        return jnp.where(lane < stripe, pltpu.roll(low, lanes - stripe, 1), pltpu.roll(edge, stripe - 4, 1))
+    return jnp.where(lane < stripe, low, pltpu.roll(edge, stripe, 1))
+
+
+def windows_of(stripe, parts):
     total = parts[0, 0]
     for m in range(1, parts.shape[0]):
         total = total + parts[m, 0]
     lats = total.shape[1]
-    for s, out in enumerate(outs):
-        turned = pltpu.roll(total, (2 - stripe * s) % lats, 1)
-        out[0] = turned[:, : out.shape[2]]
+    return [pltpu.roll(total, (2 - stripe * s) % lats, 1) for s in range(lats // stripe)]
 
 
 def adjoint_of(scale, grads, perts, lat, lon, wrapped, outs):
@@ -162,16 +182,17 @@
     return dot(high, rl_hi[...], NN) + (dot(high, rl_lo[...], NN) + dot(low, rl_hi[...], NN))
 
 
-def fine_kernel(bands, band_ref, *refs):
+def fine_kernel(bands, stripe, band_ref, *refs):
     wins, (inn, weight), consts = refs[:bands], refs[bands : bands + 2], refs[bands + 2 : bands + 8]
     outs, window = refs[bands + 8 : -1], refs[-1]
     turn, level = pl.program_id(0), pl.program_id(1)
-    width = wins[0].shape[1]
+    width = outs[0].shape[1]
     for s in range(bands):
 
         @pl.when(turn == s)
         def _():
-            window[:width, :] = wins[s][level]
+            value = wins[s][level]
+            window[:width, :] = value if value.shape[0] == width else unpacked(stripe, value, False)
 
     if width < window.shape[0]:
         window[width:, :] = jnp.zeros((window.shape[0] - width, window.shape[1]), F32)
@@ -260,28 +281,51 @@
     def swapped_spec(parts):
         return pl.BlockSpec((mates, parts, None, width, ny), lambda l, b: (0, 0, l, 0, 0))
 
-    def small_spec(parts):
-        return pl.BlockSpec((parts, None, width, lanes), lambda l, b: (0, l, 0, 0))
-
-    def stage_in(first_level, pieces, coarse):
+    def operands(view, first_level, pieces):
+        specs = [own_spec(first_level)] + [piece_spec(p[1]) for p in pieces]
+        return [view] + [p[0] for p in pieces], specs
+
+    field_spec = pl.BlockSpec((held, None, ny, nx), lambda l, b: (0, l, 0, 0))
+
+    def fields(first_level, pieces):
+        arrays, specs = operands(ctrl_view, first_level, pieces)
+
+        def kernel(band_ref, *refs):
+            for k in range(held):
+                refs[-1][k] = field_of(refs[:bands], *refs[bands : bands + 2], k)
+
+        return pl.pallas_call(
+            kernel,
+            grid_spec=scalar_grid((count,), specs + [whole_block(lat3), whole_block(lon3)], field_spec),
+            out_shape=jax.ShapeDtypeStruct((held, count, ny, nx), F32),
+            name="fields",
+        )(band_array, *arrays, lat3, lon3)
+
+    def stage_in(first_level, pieces, ready, coarse):
         arrays, specs = [], []
         if pieces is not None:
-            for at, view in enumerate((ctrl_view, mem_view)):
-                arrays += [view] + [p[0] for p in pieces[at]]
-                specs += [own_spec(first_level)] + [piece_spec(p[1]) for p in pieces[at]]
-            arrays += [lat3, lon3]
-            specs += [whole_block(lat3), whole_block(lon3)]
+            arrays, specs = operands(mem_view, first_level, pieces[1])
+            if ready is not None:
+                arrays, specs = arrays + [ready], specs + [field_spec]
+            else:
+                more, more_specs = operands(ctrl_view, first_level, pieces[0])
+                arrays += more + [lat3, lon3]
+                specs += more_specs + [whole_block(lat3), whole_block(lon3)]
         if coarse is not None:
             last = coarse[0].shape[0] - 1
             arrays += coarse
-            specs += [pl.BlockSpec((None, None, width, lanes), lambda l, b: (last, l, 0, 0))] * bands
+            specs += [pl.BlockSpec((None, None, coarse[0].shape[2], lanes), lambda l, b: (last, l, 0, 0))] * bands
         parts = (pieces is not None) + (coarse is not None)
 
         def kernel(band_ref, *refs):
             refs = list(refs)
             wrapped, out = refs.pop(), refs.pop()
             if pieces is not None:
-                fields_of(scale, refs[:bands], refs[bands : 2 * bands], *refs[2 * bands : 2 * bands + 2], wrapped, out)
+                if ready is not None:
+                    field = lambda k: refs[bands][k]
+                else:
+                    field = functools.partial(field_of, refs[bands : 2 * bands], *refs[2 * bands : 2 * bands + 2])
+                increment_of(scale, field, refs[:bands], wrapped, out)
             if coarse is not None:
                 overlapped(cy, refs[-bands:], out)
 
@@ -294,22 +338,31 @@
 
     def stage_out(swapped, fine_out):
         arrays, specs = [swapped], [swapped_spec(swapped.shape[1])]
-        parts = 1 + (fine_out is not None)
-        if fine_out is not None:
+        joined = fine_out is not None
+        tight = joined and 2 * cy == lanes
+        parts, high = (1, width + 8) if tight else (1 + joined, width)
+        if joined:
             arrays += fine_out
             specs += [pl.BlockSpec((None, None, width, lanes), lambda l, b: (0, l, 0, 0))] * bands
 
         def kernel(band_ref, *refs):
             outs = refs[len(arrays) :]
-            windows_of(cy, refs[0], outs)
-            if fine_out is not None:
-                for s in range(bands):
-                    outs[s][1] = refs[1 + (bands - s) % bands][...]
+            for s, window in enumerate(windows_of(cy, refs[0])):
+                window = window[:, :lanes]
+                result = refs[1 + (bands - s) % bands][...] if joined else None
+                if tight:
+                    outs[s][0] = packed(cy, window, result)
+                else:
+                    outs[s][0] = window
+                    if joined:
+                        outs[s][1] = result
 
         return pl.pallas_call(
             kernel,
-            grid_spec=scalar_grid((count,), specs, [small_spec(parts)] * bands),
-            out_shape=[jax.ShapeDtypeStruct((parts, count, width, lanes), F32)] * bands,
+            grid_spec=scalar_grid(
+                (count,), specs, [pl.BlockSpec((parts, None, high, lanes), lambda l, b: (0, l, 0, 0))] * bands
+            ),
+            out_shape=[jax.ShapeDtypeStruct((parts, count, high, lanes), F32)] * bands,
             name="stage_out",
         )(band_array, *arrays)
 
@@ -339,10 +392,10 @@
 
         consts = (balance, rl3, ru3, rl_hi, rl_lo, rub3)
         return pl.pallas_call(
-            functools.partial(fine_kernel, bands),
+            functools.partial(fine_kernel, bands, cy),
             grid_spec=scalar_grid(
                 (bands, count),
-                [pl.BlockSpec((None, count, width, lanes), lambda o, l, b: (0, 0, 0, 0))] * bands
+                [pl.BlockSpec((None, count, wins[0].shape[2], lanes), lambda o, l, b: (0, 0, 0, 0))] * bands
                 + [pl.BlockSpec((1, nlat, nlon), level)] * 2
                 + [whole_block(c) for c in consts],
                 [pl.BlockSpec((None, count, width, lanes), lambda o, l, b: (0, 0, 0, 0))] * bands,
@@ -372,7 +425,7 @@
     total = len(plan)
     pieces, small, result = [], None, None
     for i, (first, _) in enumerate(plan):
-        if i == 0:
+        if i in (0, total - 1):
             sides = []
             for view in (ctrl_view, mem_view):
                 sides.append([(p, 0) for p in received((view,), first)])
@@ -383,10 +436,13 @@
     for t in range(total + 2):
         now, middle, old = (i if 0 <= i < total else None for i in (t, t - 1, t - 2))
         level = None if now is None else plan[now][0]
+        ready = None
+        if now == total - 1:
+            ready = fields(level, pieces[now][0])
         coarse = None if old is None else [small[(bands - s) % bands] for s in range(bands)]
         value = None
         if now is not None or old is not None:
-            value = stage_in(level, None if now is None else pieces[now], coarse)
+            value = stage_in(level, None if now is None else pieces[now], ready, coarse)
         if value is not None:
             value = swap(value, "member")
         fine_out = None

time: 398 us -> 390 us (0.980)
  waiting for transfers between devices: 101 us -> 73.6 us
  starting transfers between devices: 162 us -> 179 us
  Pallas kernels: 95.2 us -> 101 us
    ppermute x42 -> x45, waiting for transfers between devices: 92.2 us -> 66.4 us  [shifted(): lax.ppermute(value, 'band', [(i, (i + s) % bands) for i in range(bands)])]
    ppermute x42 -> x45, starting transfers between devices: 138 us -> 156 us  [shifted(): lax.ppermute(value, 'band', [(i, (i + s) % bands) for i in range(bands)])]
    pallas_call x8 -> x9, Pallas kernels: 43.6 us -> 50.3 us  [the longest x4 37.4 us: fine(): pl.pallas_call(functools.partial(fine_kernel, bands, cy), grid_spec=scala...]
    another operation x9 -> x6, other arithmetic: 11.5 us -> 7.93 us  [sent(): return jnp.stack([lax.dynamic_slice(v, start, size)[:, 0] for v in views])]
    unnamed x131 -> x133, local copies, waits for them, and re-layouts: 10.9 us -> 11.6 us
  transfers between devices with their start and end apart: 48 -> 51, of which waited for: 17 -> 15; matrix products, arithmetic and copies ran while one was open for 5% -> 4% of each run, Pallas kernels for 20% -> 22%
where the time goes in v1:
time: 390 us; the launch traced here: 386 us
  starting transfers between devices  179 us (46%)
  Pallas kernels  101 us (26%)
  waiting for transfers between devices  73.6 us (19%)
  local copies, waits for them, and re-layouts  17.7 us (5%)
  other arithmetic  13.6 us (3%)
    ppermute x45, starting transfers between devices, shifted(): lax.ppermute(value, 'band', [(i, (i + s) % bands) for i in range(bands)])  156 us
    ppermute x45, waiting for transfers between devices, shifted(): lax.ppermute(value, 'band', [(i, (i + s) % bands) for i in range(bands)])  66.4 us
    pallas_call x4, Pallas kernels, fine(): pl.pallas_call(functools.partial(fine_kernel, bands, cy), grid_spec=scala...  37.4 us
    all_to_all x6, starting transfers between devices, body(): value = swap(value, 'member')  23.2 us
    pallas_call x6, Pallas kernels, stage_in(): pl.pallas_call(kernel, grid_spec=scalar_grid((count,), specs, swapped_spe...  22.1 us
    pallas_call x4, Pallas kernels, adjoint(): pl.pallas_call(kernel, grid_spec=scalar_grid((count,), specs, [pl.BlockSp...  18.9 us
    unnamed x133, local copies, waits for them, and re-layouts  11.6 us
    pallas_call x4, Pallas kernels, added(): pl.pallas_call(functools.partial(add_kernel, bands), grid_spec=scalar_gri...  9.49 us
  transfers between devices with their start and end apart: 51, of which 15 were waited for; matrix products, arithmetic and copies ran while one was open for 4% of the time, Pallas kernels for 22%

profile of v1, /device:TPU:0, one launch (start us, length us, event | category | flops | bytes accessed | tf_op | source)
XLA Modules:
  0.0 385.6 jit_solution(16117924638028921533)
XLA Ops:
  20.5 6.9 %collective-permute-done.16.refs_6_ = f32[1,2,1,64,512]{4,3,2,1,0:T(8,128)} collective-permute-done((f32[1,2,1,64,512]{4,3,2,1,0:T(8,128)}, f32[1,2,1,64,512]{4,3,2,1,0:T(8,128)}, u32[]{:S(2)}, u32[]{:S(2)}) %collective-permute-start.16) | collective-permute-done | bytes 262176 | tf_op jit(solution)/shard_map/ppermute | solution.py:265
  27.4 29.9 %collective-permute-start.9 = (f32[2,2,1,64,512]{4,3,2,1,0:T(8,128)}, f32[2,2,1,64,512]{4,3,2,1,0:T(8,128)S(1)}, u32[]{:S(2)}, u32[]{:S(2)}) collective-permute-start(f32[2,2,1,64,512]{4,3,2,1,0:T(8,128)} %pad_maximum_fusion.5), channel_id=1, source_target_pairs={{0,3},{1,0},{2,1},{3,2},{4,7},{5,4},{6,5},{7,6},{8,11},{9,8},{10,9... | collective-permute-start | bytes 1572872 | tf_op jit(solution)/shard_map/ppermute | solution.py:265
  61.8 4.9 %stage_in.7 = f32[8,1,1,72,256]{4,3,2,1,0:T(8,128)} custom-call(s32[1]{0:T(128)} %bitcast.band_ref, f32[2,4,4,64,512]{4,3,2,1,0:T(8,128)} %bitcast.55, f32[1,2,1,64,512]{4,3,2,1,0:T(8,128)} %copy-done.20, f32[1,2,1,64,512]{4,3,2,1,0:T(8,128)} %copy-done.19, f32[1,2,1,64,512]{4,3,2,1,0:T(8,128)} %copy-done.18, f32[2,4,4,64,512]{4,3,2,1,0:T(8,128)} %bitcast.65, ...), custom_call_target="tpu_custom_call" | custom-call | tf_op jit(solution)/shard_map/stage_in/pallas_call | solution.py:332
  72.9 18.7 %collective-permute-start.6 = (f32[2,2,1,64,512]{4,3,2,1,0:T(8,128)}, f32[2,2,1,64,512]{4,3,2,1,0:T(8,128)S(1)}, u32[]{:S(2)}, u32[]{:S(2)}) collective-permute-start(f32[2,2,1,64,512]{4,3,2,1,0:T(8,128)} %pad_maximum_fusion.2), channel_id=1, source_target_pairs={{0,3},{1,0},{2,1},{3,2},{4,7},{5,4},{6,5},{7,6},{8,11},{9,8},{10,9... | collective-permute-start | bytes 1572872 | tf_op jit(solution)/shard_map/ppermute | solution.py:265
  101.1 4.9 %stage_in.6 = f32[8,1,1,72,256]{4,3,2,1,0:T(8,128)} custom-call(s32[1]{0:T(128)} %bitcast.band_ref, f32[2,4,4,64,512]{4,3,2,1,0:T(8,128)} %bitcast.56, f32[2,2,1,64,512]{4,3,2,1,0:T(8,128)} %copy-done.3, f32[2,2,1,64,512]{4,3,2,1,0:T(8,128)} %copy-done.4, f32[2,2,1,64,512]{4,3,2,1,0:T(8,128)} %copy-done.5, f32[2,4,4,64,512]{4,3,2,1,0:T(8,128)} %bitcast.66, ...), custom_call_target="tpu_custom_call" | custom-call | tf_op jit(solution)/shard_map/stage_in/pallas_call | solution.py:332
  111.5 21.6 %collective-permute-start.18 = (f32[1,1,72,128]{3,2,1,0:T(8,128)}, f32[1,1,72,128]{3,2,1,0:T(8,128)S(1)}, u32[]{:S(2)}, u32[]{:S(2)}) collective-permute-start(f32[1,1,72,128]{3,2,1,0:T(8,128)} %get-tuple-element.54), channel_id=1, source_target_pairs={{0,1},{1,2},{2,3},{3,0},{4,5},{5,6},{6,7},{7,4},{8,9},{9,10},{10,1... | collective-permute-start | bytes 110600 | tf_op jit(solution)/shard_map/ppermute | solution.py:265
  139.8 7.1 %collective-permute-done.19.refs_2_ = f32[1,1,72,128]{3,2,1,0:T(8,128)S(1)} collective-permute-done((f32[1,1,72,128]{3,2,1,0:T(8,128)}, f32[1,1,72,128]{3,2,1,0:T(8,128)S(1)}, u32[]{:S(2)}, u32[]{:S(2)}) %collective-permute-start.19) | collective-permute-done | bytes 36896 | tf_op jit(solution)/shard_map/ppermute | solution.py:265
  148.8 8.9 %fine.4 = (f32[1,1,72,128]{3,2,1,0:T(8,128)}, f32[1,1,72,128]{3,2,1,0:T(8,128)}, f32[1,1,72,128]{3,2,1,0:T(8,128)}, f32[1,1,72,128]{3,2,1,0:T(8,128)}) custom-call(s32[1]{0:T(128)} %bitcast.band_ref, f32[1,1,72,128]{3,2,1,0:T(8,128)} %get-tuple-element.53.refs_0_, f32[1,1,72,128]{3,2,1,0:T(8,128)} %copy-done.58, f32[1,1,72,128]{3,2,1,0:T(8,128)} %copy-done.59, ...), custom_call_target="tpu_custom_call" | custom-call | tf_op jit(solution)/shard_map/fine/pallas_call | solution.py:394
  171.0 5.1 %stage_in.8 = f32[8,2,1,72,256]{4,3,2,1,0:T(8,128)} custom-call(s32[1]{0:T(128)} %bitcast.band_ref, f32[2,4,4,64,512]{4,3,2,1,0:T(8,128)} %bitcast.57, f32[2,2,1,64,512]{4,3,2,1,0:T(8,128)} %copy-done.6, f32[2,2,1,64,512]{4,3,2,1,0:T(8,128)} %copy-done.7, f32[2,2,1,64,512]{4,3,2,1,0:T(8,128)} %copy-done.8, f32[2,4,4,64,512]{4,3,2,1,0:T(8,128)} %bitcast.67, ...), custom_call_target="tpu_custom_call" | custom-call | tf_op jit(solution)/shard_map/stage_in/pallas_call | solution.py:332
  185.8 5.5 %collective-permute-done.5.refs_3_ = f32[1,2,1,64,512]{4,3,2,1,0:T(8,128)S(1)} collective-permute-done((f32[1,2,1,64,512]{4,3,2,1,0:T(8,128)}, f32[1,2,1,64,512]{4,3,2,1,0:T(8,128)S(1)}, u32[]{:S(2)}, u32[]{:S(2)}) %collective-permute-start.5) | collective-permute-done | bytes 262176 | tf_op jit(solution)/shard_map/ppermute | solution.py:265
  191.9 9.5 %fine.5 = (f32[1,1,72,128]{3,2,1,0:T(8,128)}, f32[1,1,72,128]{3,2,1,0:T(8,128)}, f32[1,1,72,128]{3,2,1,0:T(8,128)}, f32[1,1,72,128]{3,2,1,0:T(8,128)}) custom-call(s32[1]{0:T(128)} %bitcast.band_ref, f32[1,1,80,128]{3,2,1,0:T(8,128)} %get-tuple-element.61.refs_10_.refs_0_, f32[1,1,80,128]{3,2,1,0:T(8,128)} %copy-done.51, f32[1,1,80,128]{3,2,1,0:T(8,128)} %copy-done.50, ...), custom_call_target="tpu_custom_call" | custom-call | tf_op jit(solution)/shard_map/fine/pallas_call | solution.py:394
  207.5 10.4 %collective-permute-start.25 = (f32[1,1,80,128]{3,2,1,0:T(8,128)}, f32[1,1,80,128]{3,2,1,0:T(8,128)S(1)}, u32[]{:S(2)}, u32[]{:S(2)}) collective-permute-start(f32[1,1,80,128]{3,2,1,0:T(8,128)} %get-tuple-element.71), channel_id=1, source_target_pairs={{0,2},{1,3},{2,0},{3,1},{4,6},{5,7},{6,4},{7,5},{8,10},{9,11},{10,... | collective-permute-start | bytes 122888 | tf_op jit(solution)/shard_map/ppermute | solution.py:265
  217.9 5.4 %collective-permute-start.26 = (f32[1,1,80,128]{3,2,1,0:T(8,128)}, f32[1,1,80,128]{3,2,1,0:T(8,128)S(1)}, u32[]{:S(2)}, u32[]{:S(2)}) collective-permute-start(f32[1,1,80,128]{3,2,1,0:T(8,128)} %get-tuple-element.72), channel_id=1, source_target_pairs={{0,1},{1,2},{2,3},{3,0},{4,5},{5,6},{6,7},{7,4},{8,9},{9,10},{10,1... | collective-permute-start | bytes 122888 | tf_op jit(solution)/shard_map/ppermute | solution.py:265
  227.9 4.6 %collective-permute-done.25.refs_7_.refs_2_ = f32[1,1,80,128]{3,2,1,0:T(8,128)S(1)} collective-permute-done((f32[1,1,80,128]{3,2,1,0:T(8,128)}, f32[1,1,80,128]{3,2,1,0:T(8,128)S(1)}, u32[]{:S(2)}, u32[]{:S(2)}) %collective-permute-start.25) | collective-permute-done | bytes 40992 | tf_op jit(solution)/shard_map/ppermute | solution.py:265
  240.3 9.5 %fine.6 = (f32[1,1,72,128]{3,2,1,0:T(8,128)}, f32[1,1,72,128]{3,2,1,0:T(8,128)}, f32[1,1,72,128]{3,2,1,0:T(8,128)}, f32[1,1,72,128]{3,2,1,0:T(8,128)}) custom-call(s32[1]{0:T(128)} %bitcast.band_ref, f32[1,1,80,128]{3,2,1,0:T(8,128)} %get-tuple-element.69.refs_5_.refs_0_, f32[1,1,80,128]{3,2,1,0:T(8,128)} %copy-done.57, f32[1,1,80,128]{3,2,1,0:T(8,128)} %copy-done.56, ...), custom_call_target="tpu_custom_call" | custom-call | tf_op jit(solution)/shard_map/fine/pallas_call | solution.py:394
  249.8 7.2 %all-to-all-done.3.refs_0_.swap_ref = f32[8,2,1,72,256]{4,3,2,1,0:T(8,128)S(1)} async-done(((f32[8,2,1,72,256]{4,3,2,1,0:T(8,128)}), f32[8,2,1,72,256]{4,3,2,1,0:T(8,128)S(1)}, u32[]{:S(2)}, u32[]{:S(2)}) %all-to-all-start.3) | async-done | bytes 1179680 | tf_op jit(solution)/shard_map/all_to_all | solution.py:447
  274.4 9.5 %fine.7 = (f32[1,1,72,128]{3,2,1,0:T(8,128)}, f32[1,1,72,128]{3,2,1,0:T(8,128)}, f32[1,1,72,128]{3,2,1,0:T(8,128)}, f32[1,1,72,128]{3,2,1,0:T(8,128)}) custom-call(s32[1]{0:T(128)} %bitcast.band_ref, f32[1,1,80,128]{3,2,1,0:T(8,128)} %get-tuple-element.77.refs_0_, f32[1,1,80,128]{3,2,1,0:T(8,128)} %copy-done.52, f32[1,1,80,128]{3,2,1,0:T(8,128)} %copy-done.53, ...), custom_call_target="tpu_custom_call" | custom-call | tf_op jit(solution)/shard_map/fine/pallas_call | solution.py:394
  288.7 4.8 %adjoint.7 = (f32[2,1,64,512]{3,2,1,0:T(8,128)}, f32[2,1,64,512]{3,2,1,0:T(8,128)}, f32[2,1,64,512]{3,2,1,0:T(8,128)}, f32[2,1,64,512]{3,2,1,0:T(8,128)}) custom-call(s32[1]{0:T(128)} %bitcast.band_ref, f32[8,2,1,72,256]{4,3,2,1,0:T(8,128)} %copy-done.2, f32[2,4,4,64,512]{4,3,2,1,0:T(8,128)} %bitcast.59, f32[1,2,1,64,512]{4,3,2,1,0:T(8,128)} %copy-done.20, ...), custom_call_target="tpu_custom_call" | custom-call | tf_op jit(solution)/shard_map/adjoint/pallas_call | solution.py:377
  305.3 4.8 %adjoint.6 = (f32[2,1,64,512]{3,2,1,0:T(8,128)}, f32[2,1,64,512]{3,2,1,0:T(8,128)}, f32[2,1,64,512]{3,2,1,0:T(8,128)}, f32[2,1,64,512]{3,2,1,0:T(8,128)}) custom-call(s32[1]{0:T(128)} %bitcast.band_ref, f32[8,2,1,72,256]{4,3,2,1,0:T(8,128)} %copy-done.1, f32[2,4,4,64,512]{4,3,2,1,0:T(8,128)} %bitcast.60, f32[2,2,1,64,512]{4,3,2,1,0:T(8,128)} %copy-done.3, ...), custom_call_target="tpu_custom_call" | custom-call | tf_op jit(solution)/shard_map/adjoint/pallas_call | solution.py:377
  326.6 5.2 %collective-permute-start.37 = (f32[2,1,64,512]{3,2,1,0:T(8,128)}, f32[2,1,64,512]{3,2,1,0:T(8,128)S(1)}, u32[]{:S(2)}, u32[]{:S(2)}) collective-permute-start(f32[2,1,64,512]{3,2,1,0:T(8,128)} %get-tuple-element.91), channel_id=1, source_target_pairs={{0,2},{1,3},{2,0},{3,1},{4,6},{5,7},{6,4},{7,5},{8,10},{9,11},{10,... | collective-permute-start | bytes 786440 | tf_op jit(solution)/shard_map/ppermute | solution.py:265
  335.4 13.2 %collective-permute-done.40.refs_2_ = f32[2,1,64,512]{3,2,1,0:T(8,128)S(1)} collective-permute-done((f32[2,1,64,512]{3,2,1,0:T(8,128)}, f32[2,1,64,512]{3,2,1,0:T(8,128)S(1)}, u32[]{:S(2)}, u32[]{:S(2)}) %collective-permute-start.40) | collective-permute-done | bytes 262176 | tf_op jit(solution)/shard_map/ppermute | solution.py:265
  348.7 5.3 %collective-permute-start.33 = (f32[2,1,64,512]{3,2,1,0:T(8,128)}, f32[2,1,64,512]{3,2,1,0:T(8,128)S(1)}, u32[]{:S(2)}, u32[]{:S(2)}) collective-permute-start(f32[2,1,64,512]{3,2,1,0:T(8,128)} %get-tuple-element.86), channel_id=1, source_target_pairs={{0,1},{1,2},{2,3},{3,0},{4,5},{5,6},{6,7},{7,4},{8,9},{9,10},{10,1... | collective-permute-start | bytes 786440 | tf_op jit(solution)/shard_map/ppermute | solution.py:265
  362.1 9.0 %collective-permute-done.37.refs_2_ = f32[2,1,64,512]{3,2,1,0:T(8,128)S(1)} collective-permute-done((f32[2,1,64,512]{3,2,1,0:T(8,128)}, f32[2,1,64,512]{3,2,1,0:T(8,128)S(1)}, u32[]{:S(2)}, u32[]{:S(2)}) %collective-permute-start.37) | collective-permute-done | bytes 262176 | tf_op jit(solution)/shard_map/ppermute | solution.py:265
  374.3 8.1 %collective-permute-done.34.refs_2_ = f32[2,1,64,512]{3,2,1,0:T(8,128)S(1)} collective-permute-done((f32[2,1,64,512]{3,2,1,0:T(8,128)}, f32[2,1,64,512]{3,2,1,0:T(8,128)S(1)}, u32[]{:S(2)}, u32[]{:S(2)}) %collective-permute-start.34) | collective-permute-done | bytes 262176 | tf_op jit(solution)/shard_map/ppermute | solution.py:265
  (256 shorter events, 164.9 us)
Async XLA Ops:
  9.1 48.2 %collective-permute-start.15 = (f32[1,2,1,64,512]{4,3,2,1,0:T(8,128)}, f32[1,2,1,64,512]{4,3,2,1,0:T(8,128)}, u32[]{:S(2)}, u32[]{:S(2)}) collective-permute-start(f32[1,2,1,64,512]{4,3,2,1,0:T(8,128)} %get-tuple-element.105), channel_id=1, source_target_pairs={{0,3},{1,0},{2,1},{3,2},{4,7},{5,4},{6,5},{7,6},{8,11},{9,8},{10,9... | collective-permute-start | bytes 786440 | tf_op jit(solution)/shard_map/ppermute | solution.py:265
  12.1 45.1 %collective-permute-start.14 = (f32[1,2,1,64,512]{4,3,2,1,0:T(8,128)}, f32[1,2,1,64,512]{4,3,2,1,0:T(8,128)S(1)}, u32[]{:S(2)}, u32[]{:S(2)}) collective-permute-start(f32[1,2,1,64,512]{4,3,2,1,0:T(8,128)} %get-tuple-element.115), channel_id=1, source_target_pairs={{0,1},{1,2},{2,3},{3,0},{4,5},{5,6},{6,7},{7,4},{8,9},{9,10},{10,1... | collective-permute-start | bytes 786440 | tf_op jit(solution)/shard_map/ppermute | solution.py:265
  12.8 48.2 %collective-permute-start.13 = (f32[1,2,1,64,512]{4,3,2,1,0:T(8,128)}, f32[1,2,1,64,512]{4,3,2,1,0:T(8,128)S(1)}, u32[]{:S(2)}, u32[]{:S(2)}) collective-permute-start(f32[1,2,1,64,512]{4,3,2,1,0:T(8,128)} %get-tuple-element.116), channel_id=1, source_target_pairs={{0,2},{1,3},{2,0},{3,1},{4,6},{5,7},{6,4},{7,5},{8,10},{9,11},{10,... | collective-permute-start | bytes 786440 | tf_op jit(solution)/shard_map/ppermute | solution.py:265
  16.1 44.9 %collective-permute-start.12 = (f32[1,2,1,64,512]{4,3,2,1,0:T(8,128)}, f32[1,2,1,64,512]{4,3,2,1,0:T(8,128)S(1)}, u32[]{:S(2)}, u32[]{:S(2)}) collective-permute-start(f32[1,2,1,64,512]{4,3,2,1,0:T(8,128)} %get-tuple-element.117), channel_id=1, source_target_pairs={{0,3},{1,0},{2,1},{3,2},{4,7},{5,4},{6,5},{7,6},{8,11},{9,8},{10,9... | collective-permute-start | bytes 786440 | tf_op jit(solution)/shard_map/ppermute | solution.py:265
  27.4 67.8 %collective-permute-start.9 = (f32[2,2,1,64,512]{4,3,2,1,0:T(8,128)}, f32[2,2,1,64,512]{4,3,2,1,0:T(8,128)S(1)}, u32[]{:S(2)}, u32[]{:S(2)}) collective-permute-start(f32[2,2,1,64,512]{4,3,2,1,0:T(8,128)} %pad_maximum_fusion.5), channel_id=1, source_target_pairs={{0,3},{1,0},{2,1},{3,2},{4,7},{5,4},{6,5},{7,6},{8,11},{9,8},{10,9... | collective-permute-start | bytes 1572872 | tf_op jit(solution)/shard_map/ppermute | solution.py:265
  57.2 42.3 %collective-permute-start.10 = (f32[2,2,1,64,512]{4,3,2,1,0:T(8,128)}, f32[2,2,1,64,512]{4,3,2,1,0:T(8,128)S(1)}, u32[]{:S(2)}, u32[]{:S(2)}) collective-permute-start(f32[2,2,1,64,512]{4,3,2,1,0:T(8,128)} %pad_maximum_fusion.6), channel_id=1, source_target_pairs={{0,2},{1,3},{2,0},{3,1},{4,6},{5,7},{6,4},{7,5},{8,10},{9,11},{10,... | collective-permute-start | bytes 1572872 | tf_op jit(solution)/shard_map/ppermute | solution.py:265
  57.3 42.2 %collective-permute-start.11 = (f32[2,2,1,64,512]{4,3,2,1,0:T(8,128)}, f32[2,2,1,64,512]{4,3,2,1,0:T(8,128)S(1)}, u32[]{:S(2)}, u32[]{:S(2)}) collective-permute-start(f32[2,2,1,64,512]{4,3,2,1,0:T(8,128)} %pad_maximum_fusion.7), channel_id=1, source_target_pairs={{0,1},{1,2},{2,3},{3,0},{4,5},{5,6},{6,7},{7,4},{8,9},{9,10},{10,1... | collective-permute-start | bytes 1572872 | tf_op jit(solution)/shard_map/ppermute | solution.py:265
  66.7 39.2 %all-to-all-start.1 = ((f32[8,1,1,72,256]{4,3,2,1,0:T(8,128)}), f32[8,1,1,72,256]{4,3,2,1,0:T(8,128)}, u32[]{:S(2)}, u32[]{:S(2)}) async-start(f32[8,1,1,72,256]{4,3,2,1,0:T(8,128)} %stage_in.7), calls=%async_computation.1 | async-start | bytes 1179648 | tf_op jit(solution)/shard_map/all_to_all | solution.py:447
  72.9 91.5 %collective-permute-start.6 = (f32[2,2,1,64,512]{4,3,2,1,0:T(8,128)}, f32[2,2,1,64,512]{4,3,2,1,0:T(8,128)S(1)}, u32[]{:S(2)}, u32[]{:S(2)}) collective-permute-start(f32[2,2,1,64,512]{4,3,2,1,0:T(8,128)} %pad_maximum_fusion.2), channel_id=1, source_target_pairs={{0,3},{1,0},{2,1},{3,2},{4,7},{5,4},{6,5},{7,6},{8,11},{9,8},{10,9... | collective-permute-start | bytes 1572872 | tf_op jit(solution)/shard_map/ppermute | solution.py:265
  93.4 73.0 %collective-permute-start.7 = (f32[2,2,1,64,512]{4,3,2,1,0:T(8,128)}, f32[2,2,1,64,512]{4,3,2,1,0:T(8,128)S(1)}, u32[]{:S(2)}, u32[]{:S(2)}) collective-permute-start(f32[2,2,1,64,512]{4,3,2,1,0:T(8,128)} %pad_maximum_fusion.3), channel_id=1, source_target_pairs={{0,2},{1,3},{2,0},{3,1},{4,6},{5,7},{6,4},{7,5},{8,10},{9,11},{10,... | collective-permute-start | bytes 1572872 | tf_op jit(solution)/shard_map/ppermute | solution.py:265
  95.2 71.2 %collective-permute-start.8 = (f32[2,2,1,64,512]{4,3,2,1,0:T(8,128)}, f32[2,2,1,64,512]{4,3,2,1,0:T(8,128)S(1)}, u32[]{:S(2)}, u32[]{:S(2)}) collective-permute-start(f32[2,2,1,64,512]{4,3,2,1,0:T(8,128)} %pad_maximum_fusion.4), channel_id=1, source_target_pairs={{0,1},{1,2},{2,3},{3,0},{4,5},{5,6},{6,7},{7,4},{8,9},{9,10},{10,1... | collective-permute-start | bytes 1572872 | tf_op jit(solution)/shard_map/ppermute | solution.py:265
  106.0 51.7 %all-to-all-start = ((f32[8,1,1,72,256]{4,3,2,1,0:T(8,128)}), f32[8,1,1,72,256]{4,3,2,1,0:T(8,128)S(1)}, u32[]{:S(2)}, u32[]{:S(2)}) async-start(f32[8,1,1,72,256]{4,3,2,1,0:T(8,128)} %stage_in.6), calls=%async_computation | async-start | bytes 1179648 | tf_op jit(solution)/shard_map/all_to_all | solution.py:447
  181.0 26.5 %collective-permute-start.3 = (f32[1,2,1,64,512]{4,3,2,1,0:T(8,128)S(1)}, f32[1,2,1,64,512]{4,3,2,1,0:T(8,128)}, u32[]{:S(2)}, u32[]{:S(2)}) collective-permute-start(f32[1,2,1,64,512]{4,3,2,1,0:T(8,128)S(1)} %copy-done.32), channel_id=1, source_target_pairs={{0,3},{1,0},{2,1},{3,2},{4,7},{5,4},{6,5},{7,6},{8,11},{9,8},{10,9... | collective-permute-start | bytes 786440 | tf_op jit(solution)/shard_map/ppermute | solution.py:265
  183.8 34.1 %collective-permute-start.2 = (f32[1,2,1,64,512]{4,3,2,1,0:T(8,128)}, f32[1,2,1,64,512]{4,3,2,1,0:T(8,128)S(1)}, u32[]{:S(2)}, u32[]{:S(2)}) collective-permute-start(f32[1,2,1,64,512]{4,3,2,1,0:T(8,128)} %get-tuple-element.124), channel_id=1, source_target_pairs={{0,1},{1,2},{2,3},{3,0},{4,5},{5,6},{6,7},{7,4},{8,9},{9,10},{10,1... | collective-permute-start | bytes 786440 | tf_op jit(solution)/shard_map/ppermute | solution.py:265
  184.3 43.5 %collective-permute-start.1 = (f32[1,2,1,64,512]{4,3,2,1,0:T(8,128)S(1)}, f32[1,2,1,64,512]{4,3,2,1,0:T(8,128)S(1)}, u32[]{:S(2)}, u32[]{:S(2)}) collective-permute-start(f32[1,2,1,64,512]{4,3,2,1,0:T(8,128)S(1)} %copy-done.33), channel_id=1, source_target_pairs={{0,2},{1,3},{2,0},{3,1},{4,6},{5,7},{6,4},{7,5},{8,10},{9,11},{10,... | collective-permute-start | bytes 786440 | tf_op jit(solution)/shard_map/ppermute | solution.py:265
  191.9 35.9 %collective-permute-start = (f32[1,2,1,64,512]{4,3,2,1,0:T(8,128)S(1)}, f32[1,2,1,64,512]{4,3,2,1,0:T(8,128)S(1)}, u32[]{:S(2)}, u32[]{:S(2)}) collective-permute-start(f32[1,2,1,64,512]{4,3,2,1,0:T(8,128)S(1)} %copy-done.31), channel_id=1, source_target_pairs={{0,3},{1,0},{2,1},{3,2},{4,7},{5,4},{6,5},{7,6},{8,11},{9,8},{10,9... | collective-permute-start | bytes 786440 | tf_op jit(solution)/shard_map/ppermute | solution.py:265
  269.6 30.4 %all-to-all-start.5 = ((f32[8,1,1,72,256]{4,3,2,1,0:T(8,128)}), f32[8,1,1,72,256]{4,3,2,1,0:T(8,128)S(1)}, u32[]{:S(2)}, u32[]{:S(2)}) async-start(f32[8,1,1,72,256]{4,3,2,1,0:T(8,128)} %stage_in.11), calls=%async_computation.5 | async-start | bytes 1179648 | tf_op jit(solution)/shard_map/all_to_all | solution.py:447
  311.0 37.7 %collective-permute-start.40 = (f32[2,1,64,512]{3,2,1,0:T(8,128)}, f32[2,1,64,512]{3,2,1,0:T(8,128)S(1)}, u32[]{:S(2)}, u32[]{:S(2)}) collective-permute-start(f32[2,1,64,512]{3,2,1,0:T(8,128)} %get-tuple-element.95), channel_id=1, source_target_pairs={{0,2},{1,3},{2,0},{3,1},{4,6},{5,7},{6,4},{7,5},{8,10},{9,11},{10,... | collective-permute-start | bytes 786440 | tf_op jit(solution)/shard_map/ppermute | solution.py:265
  317.4 36.6 %collective-permute-start.41 = (f32[2,1,64,512]{3,2,1,0:T(8,128)S(1)}, f32[2,1,64,512]{3,2,1,0:T(8,128)S(1)}, u32[]{:S(2)}, u32[]{:S(2)}) collective-permute-start(f32[2,1,64,512]{3,2,1,0:T(8,128)S(1)} %copy-done.65), channel_id=1, source_target_pairs={{0,3},{1,0},{2,1},{3,2},{4,7},{5,4},{6,5},{7,6},{8,11},{9,8},{10,9... | collective-permute-start | bytes 786440 | tf_op jit(solution)/shard_map/ppermute | solution.py:265
  318.8 38.5 %collective-permute-start.36 = (f32[2,1,64,512]{3,2,1,0:T(8,128)}, f32[2,1,64,512]{3,2,1,0:T(8,128)S(1)}, u32[]{:S(2)}, u32[]{:S(2)}) collective-permute-start(f32[2,1,64,512]{3,2,1,0:T(8,128)} %get-tuple-element.90), channel_id=1, source_target_pairs={{0,1},{1,2},{2,3},{3,0},{4,5},{5,6},{6,7},{7,4},{8,9},{9,10},{10,1... | collective-permute-start | bytes 786440 | tf_op jit(solution)/shard_map/ppermute | solution.py:265
  326.6 44.6 %collective-permute-start.37 = (f32[2,1,64,512]{3,2,1,0:T(8,128)}, f32[2,1,64,512]{3,2,1,0:T(8,128)S(1)}, u32[]{:S(2)}, u32[]{:S(2)}) collective-permute-start(f32[2,1,64,512]{3,2,1,0:T(8,128)} %get-tuple-element.91), channel_id=1, source_target_pairs={{0,2},{1,3},{2,0},{3,1},{4,6},{5,7},{6,4},{7,5},{8,10},{9,11},{10,... | collective-permute-start | bytes 786440 | tf_op jit(solution)/shard_map/ppermute | solution.py:265
  331.8 39.4 %collective-permute-start.38 = (f32[2,1,64,512]{3,2,1,0:T(8,128)S(1)}, f32[2,1,64,512]{3,2,1,0:T(8,128)S(1)}, u32[]{:S(2)}, u32[]{:S(2)}) collective-permute-start(f32[2,1,64,512]{3,2,1,0:T(8,128)S(1)} %copy-done.64), channel_id=1, source_target_pairs={{0,3},{1,0},{2,1},{3,2},{4,7},{5,4},{6,5},{7,6},{8,11},{9,8},{10,9... | collective-permute-start | bytes 786440 | tf_op jit(solution)/shard_map/ppermute | solution.py:265
  348.7 25.7 %collective-permute-start.33 = (f32[2,1,64,512]{3,2,1,0:T(8,128)}, f32[2,1,64,512]{3,2,1,0:T(8,128)S(1)}, u32[]{:S(2)}, u32[]{:S(2)}) collective-permute-start(f32[2,1,64,512]{3,2,1,0:T(8,128)} %get-tuple-element.86), channel_id=1, source_target_pairs={{0,1},{1,2},{2,3},{3,0},{4,5},{5,6},{6,7},{7,4},{8,9},{9,10},{10,1... | collective-permute-start | bytes 786440 | tf_op jit(solution)/shard_map/ppermute | solution.py:265
  354.0 28.4 %collective-permute-start.34 = (f32[2,1,64,512]{3,2,1,0:T(8,128)}, f32[2,1,64,512]{3,2,1,0:T(8,128)S(1)}, u32[]{:S(2)}, u32[]{:S(2)}) collective-permute-start(f32[2,1,64,512]{3,2,1,0:T(8,128)} %get-tuple-element.87), channel_id=1, source_target_pairs={{0,2},{1,3},{2,0},{3,1},{4,6},{5,7},{6,4},{7,5},{8,10},{9,11},{10,... | collective-permute-start | bytes 786440 | tf_op jit(solution)/shard_map/ppermute | solution.py:265
  (93 other events, 944.5 us)

commit v2 on v1

--- a/solution.py
+++ b/solution.py
@@ -278,8 +278,8 @@
     def piece_spec(at):
         return pl.BlockSpec((None, held, None, cy, nx), lambda l, b: (at, 0, l, 0, 0))
 
-    def swapped_spec(parts):
-        return pl.BlockSpec((mates, parts, None, width, ny), lambda l, b: (0, 0, l, 0, 0))
+    def swapped_spec(parts, copies):
+        return pl.BlockSpec((copies, parts, None, width, ny), lambda l, b: (0, 0, l, 0, 0))
 
     def operands(view, first_level, pieces):
         specs = [own_spec(first_level)] + [piece_spec(p[1]) for p in pieces]
@@ -301,7 +301,7 @@
             name="fields",
         )(band_array, *arrays, lat3, lon3)
 
-    def stage_in(first_level, pieces, ready, coarse):
+    def stage_in(first_level, pieces, ready, coarse, single):
         arrays, specs = [], []
         if pieces is not None:
             arrays, specs = operands(mem_view, first_level, pieces[1])
@@ -316,6 +316,7 @@
             arrays += coarse
             specs += [pl.BlockSpec((None, None, coarse[0].shape[2], lanes), lambda l, b: (last, l, 0, 0))] * bands
         parts = (pieces is not None) + (coarse is not None)
+        copies = 1 if single else mates
 
         def kernel(band_ref, *refs):
             refs = list(refs)
@@ -331,13 +332,13 @@
 
         return pl.pallas_call(
             kernel,
-            grid_spec=scalar_grid((count,), specs, swapped_spec(parts), [wrap_scratch]),
-            out_shape=jax.ShapeDtypeStruct((mates, parts, count, width, ny), F32),
+            grid_spec=scalar_grid((count,), specs, swapped_spec(parts, copies), [wrap_scratch]),
+            out_shape=jax.ShapeDtypeStruct((copies, parts, count, width, ny), F32),
             name="stage_in",
         )(band_array, *arrays)
 
     def stage_out(swapped, fine_out):
-        arrays, specs = [swapped], [swapped_spec(swapped.shape[1])]
+        arrays, specs = [swapped], [swapped_spec(swapped.shape[1], mates)]
         joined = fine_out is not None
         tight = joined and 2 * cy == lanes
         parts, high = (1, width + 8) if tight else (1 + joined, width)
@@ -368,7 +369,7 @@
 
     def adjoint(swapped, first_level, perts):
         arrays = [swapped, mem_view] + [p[0] for p in perts] + [lat_t3, lon_b3]
-        specs = [swapped_spec(swapped.shape[1]), own_spec(first_level)] + [piece_spec(p[1]) for p in perts]
+        specs = [swapped_spec(swapped.shape[1], mates), own_spec(first_level)] + [piece_spec(p[1]) for p in perts]
         specs += [whole_block(lat_t3), whole_block(lon_b3)]
 
         def kernel(band_ref, swap_ref, *refs):
@@ -442,9 +443,12 @@
         coarse = None if old is None else [small[(bands - s) % bands] for s in range(bands)]
         value = None
         if now is not None or old is not None:
-            value = stage_in(level, None if now is None else pieces[now], ready, coarse)
+            value = stage_in(level, None if now is None else pieces[now], ready, coarse, t == total + 1)
         if value is not None:
-            value = swap(value, "member")
+            if t == total + 1:
+                value = lax.all_gather(value, "member", axis=0, tiled=True)
+            else:
+                value = swap(value, "member")
         fine_out = None
         if middle is not None:
             fine_out = fine(small, plan[middle][0])

time: 390 us -> 384 us (0.985)
  blocking collectives: 0 us -> 12.3 us
  starting transfers between devices: 179 us -> 170 us
  waiting for transfers between devices: 73.6 us -> 67.7 us
    all_gather x0 -> x1, blocking collectives: none -> 12.3 us  [body(): value = lax.all_gather(value, 'member', axis=0, tiled=True)]
    ppermute x45, waiting for transfers between devices: 66.4 us -> 60.5 us  [shifted(): lax.ppermute(value, 'band', [(i, (i + s) % bands) for i in range(bands)])]
    ppermute x45, starting transfers between devices: 156 us -> 151 us  [shifted(): lax.ppermute(value, 'band', [(i, (i + s) % bands) for i in range(bands)])]
    all_to_all x6 -> x5, starting transfers between devices: 23.2 us -> 19.1 us  [body(): value = swap(value, 'member')]
    unnamed x133 -> x135, local copies, waits for them, and re-layouts: 11.6 us -> 10.3 us
  transfers between devices with their start and end apart: 51 -> 50, of which waited for: 15 -> 15; matrix products, arithmetic and copies ran while one was open for 4% -> 4% of each run, Pallas kernels for 22% -> 22%
where the time goes in v2:
time: 384 us; the launch traced here: 381 us
  starting transfers between devices  170 us (44%)
  Pallas kernels  100 us (26%)
  waiting for transfers between devices  67.7 us (18%)
  local copies, waits for them, and re-layouts  16.5 us (4%)
  other arithmetic  13.6 us (4%)
  blocking collectives  12.3 us (3%)
    ppermute x45, starting transfers between devices, shifted(): lax.ppermute(value, 'band', [(i, (i + s) % bands) for i in range(bands)])  151 us
    ppermute x45, waiting for transfers between devices, shifted(): lax.ppermute(value, 'band', [(i, (i + s) % bands) for i in range(bands)])  60.5 us
    pallas_call x4, Pallas kernels, fine(): pl.pallas_call(functools.partial(fine_kernel, bands, cy), grid_spec=scala...  37.5 us
    pallas_call x6, Pallas kernels, stage_in(): pl.pallas_call(kernel, grid_spec=scalar_grid((count,), specs, swapped_spe...  21.8 us
    all_to_all x5, starting transfers between devices, body(): value = swap(value, 'member')  19.1 us
    pallas_call x4, Pallas kernels, adjoint(): pl.pallas_call(kernel, grid_spec=scalar_grid((count,), specs, [pl.BlockSp...  19 us
    all_gather x1, blocking collectives, body(): value = lax.all_gather(value, 'member', axis=0, tiled=True)  12.3 us
    unnamed x135, local copies, waits for them, and re-layouts  10.3 us
  transfers between devices with their start and end apart: 50, of which 15 were waited for; matrix products, arithmetic and copies ran while one was open for 4% of the time, Pallas kernels for 22%

profile of v2, /device:TPU:0, one launch (start us, length us, event | category | flops | bytes accessed | tf_op | source)
XLA Modules:
  0.0 380.8 jit_solution(11902641983404103180)
XLA Ops:
  20.5 6.9 %collective-permute-done.16.refs_6_ = f32[1,2,1,64,512]{4,3,2,1,0:T(8,128)} collective-permute-done((f32[1,2,1,64,512]{4,3,2,1,0:T(8,128)}, f32[1,2,1,64,512]{4,3,2,1,0:T(8,128)}, u32[]{:S(2)}, u32[]{:S(2)}) %collective-permute-start.16) | collective-permute-done | bytes 262176 | tf_op jit(solution)/shard_map/ppermute | solution.py:265
  27.4 29.9 %collective-permute-start.9 = (f32[2,2,1,64,512]{4,3,2,1,0:T(8,128)}, f32[2,2,1,64,512]{4,3,2,1,0:T(8,128)S(1)}, u32[]{:S(2)}, u32[]{:S(2)}) collective-permute-start(f32[2,2,1,64,512]{4,3,2,1,0:T(8,128)} %pad_maximum_fusion.5), channel_id=1, source_target_pairs={{0,3},{1,0},{2,1},{3,2},{4,7},{5,4},{6,5},{7,6},{8,11},{9,8},{10,9... | collective-permute-start | bytes 1572872 | tf_op jit(solution)/shard_map/ppermute | solution.py:265
  61.9 4.9 %stage_in.7 = f32[8,1,1,72,256]{4,3,2,1,0:T(8,128)} custom-call(s32[1]{0:T(128)} %bitcast.band_ref, f32[2,4,4,64,512]{4,3,2,1,0:T(8,128)} %bitcast.55, f32[1,2,1,64,512]{4,3,2,1,0:T(8,128)} %copy-done.19, f32[1,2,1,64,512]{4,3,2,1,0:T(8,128)} %copy-done.18, f32[1,2,1,64,512]{4,3,2,1,0:T(8,128)} %copy-done.17, f32[2,4,4,64,512]{4,3,2,1,0:T(8,128)} %bitcast.65, ...), custom_call_target="tpu_custom_call" | custom-call | tf_op jit(solution)/shard_map/stage_in/pallas_call | solution.py:333
  72.9 18.7 %collective-permute-start.6 = (f32[2,2,1,64,512]{4,3,2,1,0:T(8,128)}, f32[2,2,1,64,512]{4,3,2,1,0:T(8,128)S(1)}, u32[]{:S(2)}, u32[]{:S(2)}) collective-permute-start(f32[2,2,1,64,512]{4,3,2,1,0:T(8,128)} %pad_maximum_fusion.2), channel_id=1, source_target_pairs={{0,3},{1,0},{2,1},{3,2},{4,7},{5,4},{6,5},{7,6},{8,11},{9,8},{10,9... | collective-permute-start | bytes 1572872 | tf_op jit(solution)/shard_map/ppermute | solution.py:265
  101.1 4.9 %stage_in.6 = f32[8,1,1,72,256]{4,3,2,1,0:T(8,128)} custom-call(s32[1]{0:T(128)} %bitcast.band_ref, f32[2,4,4,64,512]{4,3,2,1,0:T(8,128)} %bitcast.56, f32[2,2,1,64,512]{4,3,2,1,0:T(8,128)} %copy-done.3, f32[2,2,1,64,512]{4,3,2,1,0:T(8,128)} %copy-done.4, f32[2,2,1,64,512]{4,3,2,1,0:T(8,128)} %copy-done.5, f32[2,4,4,64,512]{4,3,2,1,0:T(8,128)} %bitcast.66, ...), custom_call_target="tpu_custom_call" | custom-call | tf_op jit(solution)/shard_map/stage_in/pallas_call | solution.py:333
  111.6 21.6 %collective-permute-start.18 = (f32[1,1,72,128]{3,2,1,0:T(8,128)}, f32[1,1,72,128]{3,2,1,0:T(8,128)S(1)}, u32[]{:S(2)}, u32[]{:S(2)}) collective-permute-start(f32[1,1,72,128]{3,2,1,0:T(8,128)} %get-tuple-element.54), channel_id=1, source_target_pairs={{0,1},{1,2},{2,3},{3,0},{4,5},{5,6},{6,7},{7,4},{8,9},{9,10},{10,1... | collective-permute-start | bytes 110600 | tf_op jit(solution)/shard_map/ppermute | solution.py:265
  139.8 7.0 %collective-permute-done.19.refs_2_ = f32[1,1,72,128]{3,2,1,0:T(8,128)S(1)} collective-permute-done((f32[1,1,72,128]{3,2,1,0:T(8,128)}, f32[1,1,72,128]{3,2,1,0:T(8,128)S(1)}, u32[]{:S(2)}, u32[]{:S(2)}) %collective-permute-start.19) | collective-permute-done | bytes 36896 | tf_op jit(solution)/shard_map/ppermute | solution.py:265
  148.8 8.9 %fine.4 = (f32[1,1,72,128]{3,2,1,0:T(8,128)}, f32[1,1,72,128]{3,2,1,0:T(8,128)}, f32[1,1,72,128]{3,2,1,0:T(8,128)}, f32[1,1,72,128]{3,2,1,0:T(8,128)}) custom-call(s32[1]{0:T(128)} %bitcast.band_ref, f32[1,1,72,128]{3,2,1,0:T(8,128)} %get-tuple-element.53.refs_0_, f32[1,1,72,128]{3,2,1,0:T(8,128)} %copy-done.56, f32[1,1,72,128]{3,2,1,0:T(8,128)} %copy-done.57, ...), custom_call_target="tpu_custom_call" | custom-call | tf_op jit(solution)/shard_map/fine/pallas_call | solution.py:395
  171.0 5.1 %stage_in.8 = f32[8,2,1,72,256]{4,3,2,1,0:T(8,128)} custom-call(s32[1]{0:T(128)} %bitcast.band_ref, f32[2,4,4,64,512]{4,3,2,1,0:T(8,128)} %bitcast.57, f32[2,2,1,64,512]{4,3,2,1,0:T(8,128)} %copy-done.6, f32[2,2,1,64,512]{4,3,2,1,0:T(8,128)} %copy-done.7, f32[2,2,1,64,512]{4,3,2,1,0:T(8,128)} %copy-done.8, f32[2,4,4,64,512]{4,3,2,1,0:T(8,128)} %bitcast.67, ...), custom_call_target="tpu_custom_call" | custom-call | tf_op jit(solution)/shard_map/stage_in/pallas_call | solution.py:333
  185.8 5.3 %collective-permute-done.5.refs_3_ = f32[1,2,1,64,512]{4,3,2,1,0:T(8,128)S(1)} collective-permute-done((f32[1,2,1,64,512]{4,3,2,1,0:T(8,128)S(1)}, f32[1,2,1,64,512]{4,3,2,1,0:T(8,128)S(1)}, u32[]{:S(2)}, u32[]{:S(2)}) %collective-permute-start.5) | collective-permute-done | bytes 262176 | tf_op jit(solution)/shard_map/ppermute | solution.py:265
  191.0 9.6 %fine.5 = (f32[1,1,72,128]{3,2,1,0:T(8,128)}, f32[1,1,72,128]{3,2,1,0:T(8,128)}, f32[1,1,72,128]{3,2,1,0:T(8,128)}, f32[1,1,72,128]{3,2,1,0:T(8,128)}) custom-call(s32[1]{0:T(128)} %bitcast.band_ref, f32[1,1,80,128]{3,2,1,0:T(8,128)} %get-tuple-element.61.refs_10_.refs_0_, f32[1,1,80,128]{3,2,1,0:T(8,128)} %copy-done.49, f32[1,1,80,128]{3,2,1,0:T(8,128)} %copy-done.48, ...), custom_call_target="tpu_custom_call" | custom-call | tf_op jit(solution)/shard_map/fine/pallas_call | solution.py:395
  207.3 10.8 %collective-permute-start.25 = (f32[1,1,80,128]{3,2,1,0:T(8,128)}, f32[1,1,80,128]{3,2,1,0:T(8,128)S(1)}, u32[]{:S(2)}, u32[]{:S(2)}) collective-permute-start(f32[1,1,80,128]{3,2,1,0:T(8,128)} %get-tuple-element.71), channel_id=1, source_target_pairs={{0,2},{1,3},{2,0},{3,1},{4,6},{5,7},{6,4},{7,5},{8,10},{9,11},{10,... | collective-permute-start | bytes 122888 | tf_op jit(solution)/shard_map/ppermute | solution.py:265
  218.1 5.0 %collective-permute-start.26 = (f32[1,1,80,128]{3,2,1,0:T(8,128)}, f32[1,1,80,128]{3,2,1,0:T(8,128)S(1)}, u32[]{:S(2)}, u32[]{:S(2)}) collective-permute-start(f32[1,1,80,128]{3,2,1,0:T(8,128)} %get-tuple-element.72), channel_id=1, source_target_pairs={{0,1},{1,2},{2,3},{3,0},{4,5},{5,6},{6,7},{7,4},{8,9},{9,10},{10,1... | collective-permute-start | bytes 122888 | tf_op jit(solution)/shard_map/ppermute | solution.py:265
  227.6 5.0 %collective-permute-done.25.refs_7_.refs_2_ = f32[1,1,80,128]{3,2,1,0:T(8,128)S(1)} collective-permute-done((f32[1,1,80,128]{3,2,1,0:T(8,128)}, f32[1,1,80,128]{3,2,1,0:T(8,128)S(1)}, u32[]{:S(2)}, u32[]{:S(2)}) %collective-permute-start.25) | collective-permute-done | bytes 40992 | tf_op jit(solution)/shard_map/ppermute | solution.py:265
  240.5 9.5 %fine.6 = (f32[1,1,72,128]{3,2,1,0:T(8,128)}, f32[1,1,72,128]{3,2,1,0:T(8,128)}, f32[1,1,72,128]{3,2,1,0:T(8,128)}, f32[1,1,72,128]{3,2,1,0:T(8,128)}) custom-call(s32[1]{0:T(128)} %bitcast.band_ref, f32[1,1,80,128]{3,2,1,0:T(8,128)} %get-tuple-element.69.refs_5_.refs_0_, f32[1,1,80,128]{3,2,1,0:T(8,128)} %copy-done.55, f32[1,1,80,128]{3,2,1,0:T(8,128)} %copy-done.54, ...), custom_call_target="tpu_custom_call" | custom-call | tf_op jit(solution)/shard_map/fine/pallas_call | solution.py:395
  250.0 7.2 %all-to-all-done.3.refs_0_.swap_ref = f32[8,2,1,72,256]{4,3,2,1,0:T(8,128)S(1)} async-done(((f32[8,2,1,72,256]{4,3,2,1,0:T(8,128)}), f32[8,2,1,72,256]{4,3,2,1,0:T(8,128)S(1)}, u32[]{:S(2)}, u32[]{:S(2)}) %all-to-all-start.3) | async-done | bytes 1179680 | tf_op jit(solution)/shard_map/all_to_all | solution.py:451
  274.6 4.8 %adjoint.7 = (f32[2,1,64,512]{3,2,1,0:T(8,128)}, f32[2,1,64,512]{3,2,1,0:T(8,128)}, f32[2,1,64,512]{3,2,1,0:T(8,128)}, f32[2,1,64,512]{3,2,1,0:T(8,128)}) custom-call(s32[1]{0:T(128)} %bitcast.band_ref, f32[8,2,1,72,256]{4,3,2,1,0:T(8,128)} %copy-done.2, f32[2,4,4,64,512]{4,3,2,1,0:T(8,128)} %bitcast.59, f32[1,2,1,64,512]{4,3,2,1,0:T(8,128)} %copy-done.19, ...), custom_call_target="tpu_custom_call" | custom-call | tf_op jit(solution)/shard_map/adjoint/pallas_call | solution.py:378
  283.2 9.5 %fine.7 = (f32[1,1,72,128]{3,2,1,0:T(8,128)}, f32[1,1,72,128]{3,2,1,0:T(8,128)}, f32[1,1,72,128]{3,2,1,0:T(8,128)}, f32[1,1,72,128]{3,2,1,0:T(8,128)}) custom-call(s32[1]{0:T(128)} %bitcast.band_ref, f32[1,1,80,128]{3,2,1,0:T(8,128)} %get-tuple-element.77.refs_0_, f32[1,1,80,128]{3,2,1,0:T(8,128)} %copy-done.50, f32[1,1,80,128]{3,2,1,0:T(8,128)} %copy-done.51, ...), custom_call_target="tpu_custom_call" | custom-call | tf_op jit(solution)/shard_map/fine/pallas_call | solution.py:395
  295.9 4.8 %adjoint.6 = (f32[2,1,64,512]{3,2,1,0:T(8,128)}, f32[2,1,64,512]{3,2,1,0:T(8,128)}, f32[2,1,64,512]{3,2,1,0:T(8,128)}, f32[2,1,64,512]{3,2,1,0:T(8,128)}) custom-call(s32[1]{0:T(128)} %bitcast.band_ref, f32[8,2,1,72,256]{4,3,2,1,0:T(8,128)} %copy-done.1, f32[2,4,4,64,512]{4,3,2,1,0:T(8,128)} %bitcast.60, f32[2,2,1,64,512]{4,3,2,1,0:T(8,128)} %copy-done.3, ...), custom_call_target="tpu_custom_call" | custom-call | tf_op jit(solution)/shard_map/adjoint/pallas_call | solution.py:378
  315.3 12.3 %all_gather.3.swap_ref = f32[8,1,1,72,256]{4,3,2,1,0:T(8,128)} all-gather(f32[1,1,1,72,256]{4,3,2,1,0:T(8,128)} %stage_in.10), channel_id=1, replica_groups=mesh['member'=8,'band'=4] {'member'}, dimensions={0}, use_global_device_ids=true | all-gather | bytes 663552 | tf_op jit(solution)/shard_map/all_gather | solution.py:449
  327.6 4.7 %adjoint.4 = (f32[2,1,64,512]{3,2,1,0:T(8,128)}, f32[2,1,64,512]{3,2,1,0:T(8,128)}, f32[2,1,64,512]{3,2,1,0:T(8,128)}, f32[2,1,64,512]{3,2,1,0:T(8,128)}) custom-call(s32[1]{0:T(128)} %bitcast.band_ref, f32[8,1,1,72,256]{4,3,2,1,0:T(8,128)} %all_gather.3.swap_ref, f32[2,4,4,64,512]{4,3,2,1,0:T(8,128)} %bitcast.62, f32[1,2,1,64,512]{4,3,2,1,0:T(8,128)} %copy-done.29, ...), custom_call_target="tpu_custom_call" | custom-call | tf_op jit(solution)/shard_map/adjoint/pallas_call | solution.py:378
  336.0 13.5 %collective-permute-done.40.refs_2_ = f32[2,1,64,512]{3,2,1,0:T(8,128)S(1)} collective-permute-done((f32[2,1,64,512]{3,2,1,0:T(8,128)S(1)}, f32[2,1,64,512]{3,2,1,0:T(8,128)S(1)}, u32[]{:S(2)}, u32[]{:S(2)}) %collective-permute-start.40) | collective-permute-done | bytes 262176 | tf_op jit(solution)/shard_map/ppermute | solution.py:265
  349.5 5.1 %collective-permute-start.34 = (f32[2,1,64,512]{3,2,1,0:T(8,128)}, f32[2,1,64,512]{3,2,1,0:T(8,128)S(1)}, u32[]{:S(2)}, u32[]{:S(2)}) collective-permute-start(f32[2,1,64,512]{3,2,1,0:T(8,128)} %get-tuple-element.87), channel_id=1, source_target_pairs={{0,2},{1,3},{2,0},{3,1},{4,6},{5,7},{6,4},{7,5},{8,10},{9,11},{10,... | collective-permute-start | bytes 786440 | tf_op jit(solution)/shard_map/ppermute | solution.py:265
  369.5 8.1 %collective-permute-done.34.refs_2_ = f32[2,1,64,512]{3,2,1,0:T(8,128)S(1)} collective-permute-done((f32[2,1,64,512]{3,2,1,0:T(8,128)}, f32[2,1,64,512]{3,2,1,0:T(8,128)S(1)}, u32[]{:S(2)}, u32[]{:S(2)}) %collective-permute-start.34) | collective-permute-done | bytes 262176 | tf_op jit(solution)/shard_map/ppermute | solution.py:265
  (257 shorter events, 157.3 us)
Async XLA Ops:
  9.1 48.2 %collective-permute-start.15 = (f32[1,2,1,64,512]{4,3,2,1,0:T(8,128)}, f32[1,2,1,64,512]{4,3,2,1,0:T(8,128)}, u32[]{:S(2)}, u32[]{:S(2)}) collective-permute-start(f32[1,2,1,64,512]{4,3,2,1,0:T(8,128)} %get-tuple-element.105), channel_id=1, source_target_pairs={{0,3},{1,0},{2,1},{3,2},{4,7},{5,4},{6,5},{7,6},{8,11},{9,8},{10,9... | collective-permute-start | bytes 786440 | tf_op jit(solution)/shard_map/ppermute | solution.py:265
  12.2 45.1 %collective-permute-start.14 = (f32[1,2,1,64,512]{4,3,2,1,0:T(8,128)}, f32[1,2,1,64,512]{4,3,2,1,0:T(8,128)S(1)}, u32[]{:S(2)}, u32[]{:S(2)}) collective-permute-start(f32[1,2,1,64,512]{4,3,2,1,0:T(8,128)} %get-tuple-element.115), channel_id=1, source_target_pairs={{0,1},{1,2},{2,3},{3,0},{4,5},{5,6},{6,7},{7,4},{8,9},{9,10},{10,1... | collective-permute-start | bytes 786440 | tf_op jit(solution)/shard_map/ppermute | solution.py:265
  12.9 48.2 %collective-permute-start.13 = (f32[1,2,1,64,512]{4,3,2,1,0:T(8,128)}, f32[1,2,1,64,512]{4,3,2,1,0:T(8,128)S(1)}, u32[]{:S(2)}, u32[]{:S(2)}) collective-permute-start(f32[1,2,1,64,512]{4,3,2,1,0:T(8,128)} %get-tuple-element.116), channel_id=1, source_target_pairs={{0,2},{1,3},{2,0},{3,1},{4,6},{5,7},{6,4},{7,5},{8,10},{9,11},{10,... | collective-permute-start | bytes 786440 | tf_op jit(solution)/shard_map/ppermute | solution.py:265
  16.1 44.9 %collective-permute-start.12 = (f32[1,2,1,64,512]{4,3,2,1,0:T(8,128)}, f32[1,2,1,64,512]{4,3,2,1,0:T(8,128)S(1)}, u32[]{:S(2)}, u32[]{:S(2)}) collective-permute-start(f32[1,2,1,64,512]{4,3,2,1,0:T(8,128)} %get-tuple-element.117), channel_id=1, source_target_pairs={{0,3},{1,0},{2,1},{3,2},{4,7},{5,4},{6,5},{7,6},{8,11},{9,8},{10,9... | collective-permute-start | bytes 786440 | tf_op jit(solution)/shard_map/ppermute | solution.py:265
  27.4 67.8 %collective-permute-start.9 = (f32[2,2,1,64,512]{4,3,2,1,0:T(8,128)}, f32[2,2,1,64,512]{4,3,2,1,0:T(8,128)S(1)}, u32[]{:S(2)}, u32[]{:S(2)}) collective-permute-start(f32[2,2,1,64,512]{4,3,2,1,0:T(8,128)} %pad_maximum_fusion.5), channel_id=1, source_target_pairs={{0,3},{1,0},{2,1},{3,2},{4,7},{5,4},{6,5},{7,6},{8,11},{9,8},{10,9... | collective-permute-start | bytes 1572872 | tf_op jit(solution)/shard_map/ppermute | solution.py:265
  57.3 42.3 %collective-permute-start.10 = (f32[2,2,1,64,512]{4,3,2,1,0:T(8,128)}, f32[2,2,1,64,512]{4,3,2,1,0:T(8,128)S(1)}, u32[]{:S(2)}, u32[]{:S(2)}) collective-permute-start(f32[2,2,1,64,512]{4,3,2,1,0:T(8,128)} %pad_maximum_fusion.6), channel_id=1, source_target_pairs={{0,2},{1,3},{2,0},{3,1},{4,6},{5,7},{6,4},{7,5},{8,10},{9,11},{10,... | collective-permute-start | bytes 1572872 | tf_op jit(solution)/shard_map/ppermute | solution.py:265
  57.3 42.2 %collective-permute-start.11 = (f32[2,2,1,64,512]{4,3,2,1,0:T(8,128)}, f32[2,2,1,64,512]{4,3,2,1,0:T(8,128)S(1)}, u32[]{:S(2)}, u32[]{:S(2)}) collective-permute-start(f32[2,2,1,64,512]{4,3,2,1,0:T(8,128)} %pad_maximum_fusion.7), channel_id=1, source_target_pairs={{0,1},{1,2},{2,3},{3,0},{4,5},{5,6},{6,7},{7,4},{8,9},{9,10},{10,1... | collective-permute-start | bytes 1572872 | tf_op jit(solution)/shard_map/ppermute | solution.py:265
  66.8 39.2 %all-to-all-start.1 = ((f32[8,1,1,72,256]{4,3,2,1,0:T(8,128)}), f32[8,1,1,72,256]{4,3,2,1,0:T(8,128)}, u32[]{:S(2)}, u32[]{:S(2)}) async-start(f32[8,1,1,72,256]{4,3,2,1,0:T(8,128)} %stage_in.7), calls=%async_computation.1 | async-start | bytes 1179648 | tf_op jit(solution)/shard_map/all_to_all | solution.py:451
  72.9 91.5 %collective-permute-start.6 = (f32[2,2,1,64,512]{4,3,2,1,0:T(8,128)}, f32[2,2,1,64,512]{4,3,2,1,0:T(8,128)S(1)}, u32[]{:S(2)}, u32[]{:S(2)}) collective-permute-start(f32[2,2,1,64,512]{4,3,2,1,0:T(8,128)} %pad_maximum_fusion.2), channel_id=1, source_target_pairs={{0,3},{1,0},{2,1},{3,2},{4,7},{5,4},{6,5},{7,6},{8,11},{9,8},{10,9... | collective-permute-start | bytes 1572872 | tf_op jit(solution)/shard_map/ppermute | solution.py:265
  93.4 73.0 %collective-permute-start.7 = (f32[2,2,1,64,512]{4,3,2,1,0:T(8,128)}, f32[2,2,1,64,512]{4,3,2,1,0:T(8,128)S(1)}, u32[]{:S(2)}, u32[]{:S(2)}) collective-permute-start(f32[2,2,1,64,512]{4,3,2,1,0:T(8,128)} %pad_maximum_fusion.3), channel_id=1, source_target_pairs={{0,2},{1,3},{2,0},{3,1},{4,6},{5,7},{6,4},{7,5},{8,10},{9,11},{10,... | collective-permute-start | bytes 1572872 | tf_op jit(solution)/shard_map/ppermute | solution.py:265
  95.2 71.2 %collective-permute-start.8 = (f32[2,2,1,64,512]{4,3,2,1,0:T(8,128)}, f32[2,2,1,64,512]{4,3,2,1,0:T(8,128)S(1)}, u32[]{:S(2)}, u32[]{:S(2)}) collective-permute-start(f32[2,2,1,64,512]{4,3,2,1,0:T(8,128)} %pad_maximum_fusion.4), channel_id=1, source_target_pairs={{0,1},{1,2},{2,3},{3,0},{4,5},{5,6},{6,7},{7,4},{8,9},{9,10},{10,1... | collective-permute-start | bytes 1572872 | tf_op jit(solution)/shard_map/ppermute | solution.py:265
  106.0 51.7 %all-to-all-start = ((f32[8,1,1,72,256]{4,3,2,1,0:T(8,128)}), f32[8,1,1,72,256]{4,3,2,1,0:T(8,128)S(1)}, u32[]{:S(2)}, u32[]{:S(2)}) async-start(f32[8,1,1,72,256]{4,3,2,1,0:T(8,128)} %stage_in.6), calls=%async_computation | async-start | bytes 1179648 | tf_op jit(solution)/shard_map/all_to_all | solution.py:451
  183.7 34.4 %collective-permute-start.2 = (f32[1,2,1,64,512]{4,3,2,1,0:T(8,128)}, f32[1,2,1,64,512]{4,3,2,1,0:T(8,128)S(1)}, u32[]{:S(2)}, u32[]{:S(2)}) collective-permute-start(f32[1,2,1,64,512]{4,3,2,1,0:T(8,128)} %get-tuple-element.124), channel_id=1, source_target_pairs={{0,1},{1,2},{2,3},{3,0},{4,5},{5,6},{6,7},{7,4},{8,9},{9,10},{10,1... | collective-permute-start | bytes 786440 | tf_op jit(solution)/shard_map/ppermute | solution.py:265
  184.3 43.3 %collective-permute-start.1 = (f32[1,2,1,64,512]{4,3,2,1,0:T(8,128)}, f32[1,2,1,64,512]{4,3,2,1,0:T(8,128)S(1)}, u32[]{:S(2)}, u32[]{:S(2)}) collective-permute-start(f32[1,2,1,64,512]{4,3,2,1,0:T(8,128)} %get-tuple-element.125), channel_id=1, source_target_pairs={{0,2},{1,3},{2,0},{3,1},{4,6},{5,7},{6,4},{7,5},{8,10},{9,11},{10,... | collective-permute-start | bytes 786440 | tf_op jit(solution)/shard_map/ppermute | solution.py:265
  191.0 36.6 %collective-permute-start = (f32[1,2,1,64,512]{4,3,2,1,0:T(8,128)S(1)}, f32[1,2,1,64,512]{4,3,2,1,0:T(8,128)S(1)}, u32[]{:S(2)}, u32[]{:S(2)}) collective-permute-start(f32[1,2,1,64,512]{4,3,2,1,0:T(8,128)S(1)} %copy-done.30), channel_id=1, source_target_pairs={{0,3},{1,0},{2,1},{3,2},{4,7},{5,4},{6,5},{7,6},{8,11},{9,8},{10,9... | collective-permute-start | bytes 786440 | tf_op jit(solution)/shard_map/ppermute | solution.py:265
  269.8 31.0 %all-to-all-start.4 = ((f32[8,1,1,72,256]{4,3,2,1,0:T(8,128)}), f32[8,1,1,72,256]{4,3,2,1,0:T(8,128)S(1)}, u32[]{:S(2)}, u32[]{:S(2)}) async-start(f32[8,1,1,72,256]{4,3,2,1,0:T(8,128)} %stage_in.11), calls=%async_computation.4 | async-start | bytes 1179648 | tf_op jit(solution)/shard_map/all_to_all | solution.py:451
  279.4 26.7 %collective-permute-start.42 = (f32[2,1,64,512]{3,2,1,0:T(8,128)}, f32[2,1,64,512]{3,2,1,0:T(8,128)S(1)}, u32[]{:S(2)}, u32[]{:S(2)}) collective-permute-start(f32[2,1,64,512]{3,2,1,0:T(8,128)} %get-tuple-element.98), channel_id=1, source_target_pairs={{0,1},{1,2},{2,3},{3,0},{4,5},{5,6},{6,7},{7,4},{8,9},{9,10},{10,1... | collective-permute-start | bytes 786440 | tf_op jit(solution)/shard_map/ppermute | solution.py:265
  281.4 27.5 %collective-permute-start.43 = (f32[2,1,64,512]{3,2,1,0:T(8,128)}, f32[2,1,64,512]{3,2,1,0:T(8,128)S(1)}, u32[]{:S(2)}, u32[]{:S(2)}) collective-permute-start(f32[2,1,64,512]{3,2,1,0:T(8,128)} %get-tuple-element.99), channel_id=1, source_target_pairs={{0,2},{1,3},{2,0},{3,1},{4,6},{5,7},{6,4},{7,5},{8,10},{9,11},{10,... | collective-permute-start | bytes 786440 | tf_op jit(solution)/shard_map/ppermute | solution.py:265
  309.0 40.5 %collective-permute-start.40 = (f32[2,1,64,512]{3,2,1,0:T(8,128)S(1)}, f32[2,1,64,512]{3,2,1,0:T(8,128)S(1)}, u32[]{:S(2)}, u32[]{:S(2)}) collective-permute-start(f32[2,1,64,512]{3,2,1,0:T(8,128)S(1)} %copy-done.66), channel_id=1, source_target_pairs={{0,2},{1,3},{2,0},{3,1},{4,6},{5,7},{6,4},{7,5},{8,10},{9,11},{10,... | collective-permute-start | bytes 786440 | tf_op jit(solution)/shard_map/ppermute | solution.py:265
  310.1 39.4 %collective-permute-start.41 = (f32[2,1,64,512]{3,2,1,0:T(8,128)S(1)}, f32[2,1,64,512]{3,2,1,0:T(8,128)S(1)}, u32[]{:S(2)}, u32[]{:S(2)}) collective-permute-start(f32[2,1,64,512]{3,2,1,0:T(8,128)S(1)} %copy-done.65), channel_id=1, source_target_pairs={{0,3},{1,0},{2,1},{3,2},{4,7},{5,4},{6,5},{7,6},{8,11},{9,8},{10,9... | collective-permute-start | bytes 786440 | tf_op jit(solution)/shard_map/ppermute | solution.py:265
  312.9 41.7 %collective-permute-start.36 = (f32[2,1,64,512]{3,2,1,0:T(8,128)}, f32[2,1,64,512]{3,2,1,0:T(8,128)S(1)}, u32[]{:S(2)}, u32[]{:S(2)}) collective-permute-start(f32[2,1,64,512]{3,2,1,0:T(8,128)} %get-tuple-element.90), channel_id=1, source_target_pairs={{0,1},{1,2},{2,3},{3,0},{4,5},{5,6},{6,7},{7,4},{8,9},{9,10},{10,1... | collective-permute-start | bytes 786440 | tf_op jit(solution)/shard_map/ppermute | solution.py:265
  332.4 37.2 %collective-permute-start.33 = (f32[2,1,64,512]{3,2,1,0:T(8,128)}, f32[2,1,64,512]{3,2,1,0:T(8,128)S(1)}, u32[]{:S(2)}, u32[]{:S(2)}) collective-permute-start(f32[2,1,64,512]{3,2,1,0:T(8,128)} %get-tuple-element.86), channel_id=1, source_target_pairs={{0,1},{1,2},{2,3},{3,0},{4,5},{5,6},{6,7},{7,4},{8,9},{9,10},{10,1... | collective-permute-start | bytes 786440 | tf_op jit(solution)/shard_map/ppermute | solution.py:265
  334.1 32.3 %collective-permute-start.37 = (f32[2,1,64,512]{3,2,1,0:T(8,128)S(1)}, f32[2,1,64,512]{3,2,1,0:T(8,128)S(1)}, u32[]{:S(2)}, u32[]{:S(2)}) collective-permute-start(f32[2,1,64,512]{3,2,1,0:T(8,128)S(1)} %copy-done.64), channel_id=1, source_target_pairs={{0,2},{1,3},{2,0},{3,1},{4,6},{5,7},{6,4},{7,5},{8,10},{9,11},{10,... | collective-permute-start | bytes 786440 | tf_op jit(solution)/shard_map/ppermute | solution.py:265
  349.5 28.1 %collective-permute-start.34 = (f32[2,1,64,512]{3,2,1,0:T(8,128)}, f32[2,1,64,512]{3,2,1,0:T(8,128)S(1)}, u32[]{:S(2)}, u32[]{:S(2)}) collective-permute-start(f32[2,1,64,512]{3,2,1,0:T(8,128)} %get-tuple-element.87), channel_id=1, source_target_pairs={{0,2},{1,3},{2,0},{3,1},{4,6},{5,7},{6,4},{7,5},{8,10},{9,11},{10,... | collective-permute-start | bytes 786440 | tf_op jit(solution)/shard_map/ppermute | solution.py:265
  (93 other events, 939.0 us)
